TPU v7x, 512 devices: a whole 4x8x8 slice. The times are simulated.
512 devices in a mesh: row: 4 (over x), col: 16 (over y_lo, z), aux: 8 (over y_hi, core).
Axes of the slice: x: 4, y: 8 (y_hi: 4, y_lo: 2; y = y_hi * 2 + y_lo), z: 8, core: 2. Of those that a mesh axis runs over, the one named last changes fastest.
Arguments:
- green_occ: bfloat16 [4096, 4096], P('row', 'col'), may hold values from -6 to 6
- green_virt: bfloat16 [4096, 4096], P('row', 'col'), may hold values from -0.09375 to 0.09375
- integrals: bfloat16 [4, 16, 256, 8, 4096], P('row', 'col', 'aux'), may hold values from -0.0625 to 0.0625
- listed_tile_index: int32 [4, 16, 8, 8], P('row', 'col', 'aux'), may hold values from 0 to 63, as said below
- metric: float32 [256, 256], P('aux'), may hold values from -0.375 to 0.375
Outputs:
- product: bfloat16 [4096, 4096], P('row', 'col')
- aux_coeff: float32 [256], P('aux')
- occ_force: float32 [4096, 4096], P('col', ('row', 'aux'))
Inputs may be any that keep to these rules, and one draw needn't show every extreme that they name: Each entry of listed_tile_index[r, c, a] is a distinct tile of tile (r, c). Aux owner o holds block rows o * 2 to (o + 1) * 2 - 1 of every tile; each list names exactly 2 tiles in each of 4 owners and none in the others. In every tile (r, c) one owner receives 2 tiles from every aux index.
All inputs are finite; a program needn't handle non-finite values.
Results may differ from a plain program's by a relative error of at most 0.0048.
Values may be sent and summed in bfloat16 or wider, within the bound.
A program may use at most 64 MiB of HBM per device.

v0:
```python
import math

import jax
import jax.numpy as jnp
from jax import lax
from jax.sharding import Mesh
from jax.sharding import PartitionSpec as P

BLK = 64
CAP = 2
AUX = ("aux_0", "aux_1")
COL = ("col_0", "col_1")
ROW_COL_AUX = ("row", "col_0", "col_1", "aux_0", "aux_1")
ROW_AUX = ("row", "aux_0", "aux_1")


def laid_out(pieces, dim):
    lengths = list(pieces.shape[1:])
    lengths[dim] *= pieces.shape[0]
    return jnp.moveaxis(pieces, 0, dim).reshape(lengths)


def from_everyone(x, axis):
    count = lax.axis_size(axis)
    return lax.all_to_all(jnp.broadcast_to(x[None], (count, *x.shape)), axis, 0, 0, tiled=True)


def gather_directly(x, axis, dim):
    return laid_out(from_everyone(x, axis), dim)


def over_axes(x, axes):
    for axis in axes:
        x = lax.psum(x, axis)
    return x


def side_by_side(arrays, axis, split_dim, concat_dim, along):
    widths = [math.prod(a.shape[along:]) for a in arrays]
    both = jnp.concatenate(
        [a.reshape(*a.shape[:along], w) for a, w in zip(arrays, widths)], axis=along
    )
    out = lax.all_to_all(both, axis, split_axis=split_dim, concat_axis=concat_dim, tiled=True)
    pieces = jnp.split(out, [sum(widths[:k]) for k in range(1, len(widths))], axis=along)
    return tuple((b.reshape(*out.shape[:along], *a.shape[along:]) for a, b in zip(arrays, pieces)))


def cut_along(x, dim, count):
    lengths = x.shape
    pieces = x.reshape(*lengths[:dim], count, lengths[dim] // count, *lengths[dim + 1 :])
    return jnp.moveaxis(pieces, dim, 0)


def sent_and_summed(x, axis, dim):
    pieces = cut_along(x, dim, lax.axis_size(axis))
    arrived = lax.all_to_all(pieces, axis, split_axis=0, concat_axis=0, tiled=True)
    return arrived.sum(axis=0)


def on_device(green_occ, green_virt, integrals, listed_tile_index, metric):
    block_width = BLK
    listed_count = listed_tile_index.shape[-1]
    aux_count = lax.axis_size(AUX)
    aux_local = integrals.shape[2]
    tile_height = green_occ.shape[0]
    tile_width = green_occ.shape[1]
    owner_height = tile_height // aux_count
    aux_here = lax.axis_index(AUX)
    virtual = lax.all_gather(green_virt, "row", axis=0, tiled=True)
    owner_part = lax.dynamic_slice_in_dim(green_occ, aux_here * owner_height, owner_height, 0)
    partial_rows = jnp.dot(
        gather_directly(owner_part, COL, 1), virtual, preferred_element_type=jnp.float32
    )
    product = gather_directly(partial_rows.astype(jnp.bfloat16), AUX, 0)
    block_rows = tile_height // block_width
    block_cols = tile_width // block_width
    tile_count = block_rows * block_cols
    flat_size = block_width * block_width
    tiles = product.reshape(block_rows, block_width, block_cols, block_width).transpose(0, 2, 1, 3)
    tiles = tiles.reshape(tile_count, flat_size)
    listed = listed_tile_index.reshape(listed_count)
    selector = (listed[:, None] == jnp.arange(tile_count, dtype=jnp.int32)[None, :]).astype(
        jnp.bfloat16
    )
    chosen = jnp.dot(selector, tiles, preferred_element_type=jnp.float32).astype(jnp.bfloat16)
    local_ints = integrals.reshape(aux_local, listed_count, flat_size)
    partial_coeff = lax.dot_general(
        local_ints, chosen, (((1, 2), (0, 1)), ((), ())), preferred_element_type=jnp.float32
    )
    spread_coeff = jnp.zeros((aux_count * aux_local,), jnp.float32)
    spread_coeff = lax.dynamic_update_slice_in_dim(
        spread_coeff, partial_coeff, aux_here * aux_local, 0
    )
    fitting_coefficients = over_axes(spread_coeff, ROW_COL_AUX)
    own_coeff = lax.dynamic_slice_in_dim(fitting_coefficients, aux_here * aux_local, aux_local, 0)
    screened_blocks = jnp.dot(metric, fitting_coefficients, precision=lax.Precision.HIGHEST)
    block_values = jnp.dot(
        screened_blocks,
        local_ints.reshape(aux_local, listed_count * flat_size),
        precision=lax.Precision.HIGHEST,
        preferred_element_type=jnp.float32,
    )
    block_values = block_values.reshape(listed_count, flat_size)
    owner_tiles = block_rows // aux_count * block_cols
    owner_of = listed // owner_tiles
    positions = jnp.arange(listed_count, dtype=jnp.int32)
    same_owner = owner_of[:, None] == owner_of[None, :]
    earlier = positions[:, None] > positions[None, :]
    rank = jnp.sum((same_owner & earlier).astype(jnp.int32), axis=1)
    slot = owner_of * CAP + rank
    slot_table = (slot[None, :] == jnp.arange(aux_count * CAP, dtype=jnp.int32)[:, None]).astype(
        jnp.float32
    )
    outgoing = jnp.dot(slot_table, block_values, precision=lax.Precision.HIGHEST).reshape(
        aux_count, CAP, flat_size
    )
    labels = (
        jnp.dot(slot_table, (listed + 1).astype(jnp.float32), precision=lax.Precision.HIGHEST) - 1.0
    )
    labels = labels.reshape(aux_count, CAP)
    received_blocks, arrived_labels = side_by_side((outgoing, labels), AUX, 0, 0, 2)
    local_label = arrived_labels.reshape(aux_count * CAP).astype(jnp.int32) - aux_here * owner_tiles
    placement = (jnp.arange(owner_tiles, dtype=jnp.int32)[:, None] == local_label[None, :]).astype(
        jnp.float32
    )
    owned = jnp.dot(
        placement,
        received_blocks.reshape(aux_count * CAP, flat_size),
        precision=lax.Precision.HIGHEST,
    )
    owned = owned.reshape(block_rows // aux_count, block_cols, block_width, block_width).transpose(
        0, 2, 1, 3
    )
    owned = owned.reshape(owner_height, tile_width)
    derivative = owned.astype(jnp.bfloat16)
    occ_force = sent_and_summed(
        lax.dot_general(
            virtual, derivative, (((1,), (1,)), ((), ())), preferred_element_type=jnp.float32
        ),
        COL,
        0,
    )
    return (product, own_coeff, occ_force)


def solution(mesh):
    split = Mesh(
        mesh.devices.reshape(mesh.shape["row"], 2, 8, 4, 2),
        ("row", "col_0", "col_1", "aux_0", "aux_1"),
    )
    return jax.shard_map(
        on_device,
        mesh=split,
        in_specs=(
            P("row", COL),
            P("row", COL),
            P("row", COL, AUX, None, None),
            P("row", COL, AUX, None),
            P(AUX, None),
        ),
        out_specs=(P("row", COL), P(AUX), P(COL, ROW_AUX)),
        check_vma=False,
    )
```

profile of v0, /device:TPU:8, one launch (start us, length us, event | category | flops | bytes accessed | tf_op | source)
XLA Modules:
  0.0 222.6 jit_solution(14527885088304888355)
XLA Ops:
  7.2 0.7 all-gather.2.cloned.1.call-update
  7.9 0.3 copy-done
  8.2 0.1 copy.37
  8.3 0.2 broadcast_in_dim.6
  8.5 37.7 %all_to_all.20 = bf16[16,128,256]{1,2,0:T(8,128)(2,1)S(1)} all-to-all(bf16[16,128,256]{1,2,0:T(8,128)(2,1)S(1)} %broadcast_in_dim.6), channel_id=1, replica_groups=mesh['row'=4,'col_0'=2,'col_1'=8,'aux_0'=4,'aux_1'=2] {'col_0','col_1'}, dimensions={0} | all-to-all | bytes 2097152 | tf_op jit(solution)/shard_map/all_to_all | solution.py:25
  46.3 4.5 %all-gather.2.cloned.1.call-done = bf16[4096,256]{1,0:T(8,128)(2,1)} async-done(((bf16[1024,256]{1,0:T(8,128)(2,1)}), bf16[4096,256]{1,0:T(8,128)(2,1)}) %all-gather.2.cloned.1.call-update) | async-done | bytes 2097168 | tf_op jit(solution)/shard_map/all_gather | solution.py:69
  50.8 2.2 convolution_convert_fusion.2
  53.0 0.1 copy.38
  53.1 0.9 broadcast_in_dim.7
  54.0 5.8 %all-to-all-start.1 = ((bf16[8,128,256]{1,2,0:T(8,128)(2,1)}), bf16[8,128,256]{1,2,0:T(8,128)(2,1)S(1)}, u32[]{:S(2)}, u32[]{:S(2)}) async-start(bf16[8,128,256]{1,2,0:T(8,128)(2,1)} %broadcast_in_dim.7), calls=%async_computation.1 | async-start | bytes 1048576 | tf_op jit(solution)/shard_map/all_to_all | solution.py:25
  59.8 0.2 convert_reduce_fusion
  60.0 0.1 fusion.7
  60.1 0.1 reshape_reshape.13
  60.2 17.9 %all-to-all-done.1 = bf16[8,128,256]{1,2,0:T(8,128)(2,1)S(1)} async-done(((bf16[8,128,256]{1,2,0:T(8,128)(2,1)}), bf16[8,128,256]{1,2,0:T(8,128)(2,1)S(1)}, u32[]{:S(2)}, u32[]{:S(2)}) %all-to-all-start.1) | async-done | bytes 524320 | tf_op jit(solution)/shard_map/all_to_all | solution.py:25
  78.1 0.3 copy.40
  78.5 0.4 reshape_reshape.10
  78.9 1.0 copy.41
  79.9 0.8 reshape.135
  80.7 0.2 fusion
  80.9 4.2 %fusion.8 = f32[32]{0:T(128)S(1)} fusion(bf16[32,8,4096]{2,1,0:T(8,128)(2,1)} %bitcast.83, bf16[8,4096,1]{1,0,2:T(8,128)(2,1)S(1)} %fusion), kind=kOutput, calls=%fused_computation.14 | convolution fusion | flops 2097152 | bytes 2162816 | tf_op jit(solution)/shard_map/dot_general | solution.py:87
  85.2 0.2 dynamic_update_slice.3
  85.4 8.6 %psum.35 = f32[256]{0:T(256)S(1)} all-reduce(f32[256]{0:T(256)S(1)} %dynamic_update_slice.3), channel_id=1, replica_groups=mesh['row'=4,'col_0'=2,'col_1'=8,'aux_0'=4,'aux_1'=2] {'row'}, use_global_device_ids=true, to_apply=%region_0.0 | all-reduce | flops 256 | bytes 2048 | tf_op jit(solution)/shard_map/psum | solution.py:34
  93.9 4.9 %psum.36 = f32[256]{0:T(256)S(1)} all-reduce(f32[256]{0:T(256)S(1)} %psum.35), channel_id=1, replica_groups=mesh['row'=4,'col_0'=2,'col_1'=8,'aux_0'=4,'aux_1'=2] {'col_0'}, use_global_device_ids=true, to_apply=%region_1.0 | all-reduce | flops 256 | bytes 2048 | tf_op jit(solution)/shard_map/psum | solution.py:34
  98.9 18.1 %psum.37 = f32[256]{0:T(256)S(1)} all-reduce(f32[256]{0:T(256)S(1)} %psum.36), channel_id=1, replica_groups=mesh['row'=4,'col_0'=2,'col_1'=8,'aux_0'=4,'aux_1'=2] {'col_1'}, use_global_device_ids=true, to_apply=%region_2.0 | all-reduce | flops 256 | bytes 2048 | tf_op jit(solution)/shard_map/psum | solution.py:34
  116.9 9.2 %psum.38 = f32[256]{0:T(256)S(1)} all-reduce(f32[256]{0:T(256)S(1)} %psum.37), channel_id=1, replica_groups=mesh['row'=4,'col_0'=2,'col_1'=8,'aux_0'=4,'aux_1'=2] {'aux_0'}, use_global_device_ids=true, to_apply=%region_3.0 | all-reduce | flops 256 | bytes 2048 | tf_op jit(solution)/shard_map/psum | solution.py:34
  126.1 2.5 %psum.39 = f32[256]{0:T(256)S(1)} all-reduce(f32[256]{0:T(256)S(1)} %psum.38), channel_id=1, replica_groups=mesh['row'=4,'col_0'=2,'col_1'=8,'aux_0'=4,'aux_1'=2] {'aux_1'}, use_global_device_ids=true, to_apply=%region_4.0 | all-reduce | flops 256 | bytes 2048 | tf_op jit(solution)/shard_map/psum | solution.py:34
  128.6 0.1 convolution_bitcast_fusion
  128.7 3.0 %fusion.1 = f32[1,8,4096]{2,0,1:T(1,128)S(1)} fusion(f32[32,1,1]{0,1,2:T(1,128)S(1)} %convolution_bitcast_fusion, bf16[4,8,8,4096]{3,2,1,0:T(8,128)(2,1)S(1)} %bitcast.84), kind=kOutput, calls=%fused_computation.3 | convolution fusion | flops 12582912 | bytes 2228352 | tf_op jit(solution)/shard_map/dot_general | solution.py:97
  131.7 0.3 fusion.13
  132.0 0.9 reshape.137
  132.9 1.8 pad_maximum_fusion
  134.7 4.2 %all-to-all-start.2 = ((f32[8,2,4097]{2,1,0:T(2,128)}), f32[8,2,4097]{2,1,0:T(2,128)S(1)}, u32[]{:S(2)}, u32[]{:S(2)}) async-start(f32[8,2,4097]{2,1,0:T(2,128)} %pad_maximum_fusion), calls=%async_computation.2 | async-start | bytes 540672 | tf_op jit(solution)/shard_map/all_to_all | solution.py:43
  138.9 12.9 %all-to-all-done.2 = f32[8,2,4097]{2,1,0:T(2,128)S(1)} async-done(((f32[8,2,4097]{2,1,0:T(2,128)}), f32[8,2,4097]{2,1,0:T(2,128)S(1)}, u32[]{:S(2)}, u32[]{:S(2)}) %all-to-all-start.2) | async-done | bytes 262240 | tf_op jit(solution)/shard_map/all_to_all | solution.py:43
  151.8 0.2 fusion.18
  152.0 0.1 sub.24
  152.0 0.7 split.9
  152.8 1.1 reshape.138
  153.9 1.0 dot_general.47
  154.9 1.7 fusion.6
  156.6 0.1 convert_element_type.39
  156.8 0.8 fusion.31
  157.6 1.6 copy.78
  159.1 5.6 %all-to-all-start.3 = ((f32[16,256,128]{1,2,0:T(8,128)}), f32[16,256,128]{1,2,0:T(8,128)S(1)}, u32[]{:S(2)}, u32[]{:S(2)}) async-start(f32[16,256,128]{1,2,0:T(8,128)} %bitcast.75), calls=%async_computation.3 | async-start | bytes 4194304 | tf_op jit(solution)/shard_map/all_to_all | solution.py:56
  164.8 0.6 dynamic_slice.7
  165.4 1.0 copy.39
  166.4 48.5 %all-to-all-done.3 = f32[16,256,128]{1,2,0:T(8,128)S(1)} async-done(((f32[16,256,128]{1,2,0:T(8,128)}), f32[16,256,128]{1,2,0:T(8,128)S(1)}, u32[]{:S(2)}, u32[]{:S(2)}) %all-to-all-start.3) | async-done | bytes 2097184 | tf_op jit(solution)/shard_map/all_to_all | solution.py:56
  214.8 0.1 reduce_sum.19
  215.0 0.8 copy.46
  (15 shorter events, 0.1 us)
Async XLA Ops:
  7.2 1.0 copy-start
  7.2 43.6 %all-gather.2.cloned.1.call-start = ((), (), s32[]{:S(2)}) async-start(), calls=%async_computation.4 | async-start | bytes 2621440 | tf_op jit(solution)/shard_map/all_gather | solution.py:69
  50.8 9.0 %copy-start.3 = (s32[1,1,1,8]{3,2,1,0:T(1,128)S(1)}, s32[1,1,1,8]{3,2,1,0:T(1,128)}, u32[]{:S(2)}) copy-start(s32[1,1,1,8]{3,2,1,0:T(1,128)} %param.8) | copy-start | bytes 100
  54.0 24.2 %all-to-all-start.1 = ((bf16[8,128,256]{1,2,0:T(8,128)(2,1)}), bf16[8,128,256]{1,2,0:T(8,128)(2,1)S(1)}, u32[]{:S(2)}, u32[]{:S(2)}) async-start(bf16[8,128,256]{1,2,0:T(8,128)(2,1)} %broadcast_in_dim.7), calls=%async_computation.1 | async-start | bytes 1048576 | tf_op jit(solution)/shard_map/all_to_all | solution.py:25
  79.9 48.7 %copy-start.2 = (f32[32,256]{1,0:T(8,128)S(1)}, f32[32,256]{1,0:T(8,128)}, u32[]{:S(2)}) copy-start(f32[32,256]{1,0:T(8,128)} %param.9) | copy-start | bytes 98308
  80.9 47.8 %copy-start.4 = (bf16[1,1,32,8,4096]{4,3,2,1,0:T(8,128)(2,1)S(1)}, bf16[1,1,32,8,4096]{4,3,2,1,0:T(8,128)(2,1)}, u32[]{:S(2)}) copy-start(bf16[1,1,32,8,4096]{4,3,2,1,0:T(8,128)(2,1)} %param.7) | copy-start | bytes 6291460
  132.0 24.8 %copy-start.1 = (bf16[4096,256]{1,0:T(8,128)(2,1)S(1)}, bf16[4096,256]{1,0:T(8,128)(2,1)}, u32[]{:S(2)}) copy-start(bf16[4096,256]{1,0:T(8,128)(2,1)} %all-gather.2.cloned.1.call-done) | copy-start | bytes 6291460
  134.7 17.1 %all-to-all-start.2 = ((f32[8,2,4097]{2,1,0:T(2,128)}), f32[8,2,4097]{2,1,0:T(2,128)S(1)}, u32[]{:S(2)}, u32[]{:S(2)}) async-start(f32[8,2,4097]{2,1,0:T(2,128)} %pad_maximum_fusion), calls=%async_computation.2 | async-start | bytes 540672 | tf_op jit(solution)/shard_map/all_to_all | solution.py:43
  159.1 55.7 %all-to-all-start.3 = ((f32[16,256,128]{1,2,0:T(8,128)}), f32[16,256,128]{1,2,0:T(8,128)S(1)}, u32[]{:S(2)}, u32[]{:S(2)}) async-start(f32[16,256,128]{1,2,0:T(8,128)} %bitcast.75), calls=%async_computation.3 | async-start | bytes 4194304 | tf_op jit(solution)/shard_map/all_to_all | solution.py:56
Sparse Core Ops, SparseCore 0:
  10.1 40.6 all-gather.1
where the time goes:
time: 223 us
  waiting for transfers between devices  84.4 us (38%)
  blocking collectives  80.9 us (36%)
  starting transfers between devices  15.7 us (7%)
  between operations  14.2 us (6%)
  matrix products  12.6 us (6%)
  local copies, waits for them, and re-layouts  12.3 us (6%)
  other arithmetic  2.33 us (1%)
    all_to_all x1, waiting for transfers between devices, sent_and_summed(): lax.all_to_all(pieces, axis, split_axis=0, concat_axis=0, tiled=True)  48.5 us
    psum x5, blocking collectives, over_axes(): x = lax.psum(x, axis)  43.2 us
    all_to_all x1, blocking collectives, from_everyone(): lax.all_to_all(jnp.broadcast_to(x[None], (count, *x.shape)), axis, 0, 0,...  37.7 us
    all_to_all x1, waiting for transfers between devices, from_everyone(): lax.all_to_all(jnp.broadcast_to(x[None], (count, *x.shape)), axis, 0, 0,...  17.9 us
    all_to_all x1, waiting for transfers between devices, side_by_side(): lax.all_to_all(both, axis, split_axis=split_dim, concat_axis=concat_dim,...  12.9 us
    all_to_all x1, starting transfers between devices, from_everyone(): lax.all_to_all(jnp.broadcast_to(x[None], (count, *x.shape)), axis, 0, 0,...  5.84 us
    all_to_all x1, starting transfers between devices, sent_and_summed(): lax.all_to_all(pieces, axis, split_axis=0, concat_axis=0, tiled=True)  5.64 us
    all_gather x1, waiting for transfers between devices, on_device(): virtual = lax.all_gather(green_virt, 'row', axis=0, tiled=True)  4.5 us
  transfers between devices with their start and end apart: 4, of which 4 were waited for; matrix products, arithmetic and copies ran while one was open for 1% of the time, Pallas kernels for 0%

commit v1 on v0

v1 whole, which is shorter than its diff:
```python
import jax
import jax.numpy as jnp
from jax import lax
from jax.experimental import pallas as pl
from jax.experimental.pallas import tpu as pltpu
from jax.sharding import Mesh
from jax.sharding import PartitionSpec as P

MESH = pl.DeviceIdType.MESH
BF = jnp.bfloat16
F32 = jnp.float32
NX, NYL, NZ, NYH, NCO = 4, 2, 8, 4, 2
NCOPY = 144


def iota(shape, dim):
    return lax.broadcasted_iota(jnp.int32, shape, dim)


def rows_from_tiles(fl, rows):
    left = iota((32, 128), 1) < 64
    for br in range(2):
        for q in range(2):
            t = br * 4 + 2 * q
            a = fl[pl.ds(t, 32, stride=8), :]
            b = fl[pl.ds(t + 1, 32, stride=8), :]
            even = jnp.where(left, a, pltpu.roll(b, 64, 1))
            odd = jnp.where(left, pltpu.roll(a, 64, 1), b)
            rows[q, pl.ds(br * 64, 32, stride=2), :] = even
            rows[q, pl.ds(br * 64 + 1, 32, stride=2), :] = odd


def tiles_from_rows(rows, fl):
    left = iota((32, 128), 1) < 64
    for br in range(2):
        for q in range(2):
            t = br * 4 + 2 * q
            even = rows[q, pl.ds(br * 64, 32, stride=2), :]
            odd = rows[q, pl.ds(br * 64 + 1, 32, stride=2), :]
            fl[pl.ds(t, 32, stride=8), :] = jnp.where(left, even, pltpu.roll(odd, 64, 1))
            fl[pl.ds(t + 1, 32, stride=8), :] = jnp.where(left, pltpu.roll(even, 64, 1), odd)


def body(
    listed, occ, virt, ints, metric, prod_out, coeff_out, force_out,
    VIRT, OCC, AV, FL, ROWS, TILES, TF, CSRC, CZ, CX, CY, ACC, SCB, LSRC, LB,
    BV, SB, RB, FP, SH, RH, SF, RF, SY, RY, SP, RP, ssem, rsem, lsem,
):
    x = lax.axis_index("row")
    yl = lax.axis_index("ylo")
    z = lax.axis_index("z")
    yh = lax.axis_index("yhi")
    co = lax.axis_index("core")
    a = yh * 2 + co
    count = [0]
    started = []

    def send(src, dst, **to):
        k = count[0]
        count[0] += 1
        c = pltpu.make_async_remote_copy(
            src_ref=src, dst_ref=dst, send_sem=ssem.at[k], recv_sem=rsem.at[k],
            device_id=to, device_id_type=MESH,
        )
        c.start()
        started.append(c)
        return c

    def shift(axis, n, me, d):
        return {axis: lax.rem(me + d + n, n)}

    def ypeers():
        for dl in range(NYL):
            for dh in range(NYH):
                for dc in range(NCO):
                    if dl or dh or dc:
                        yield {
                            "ylo": lax.rem(yl + dl, NYL),
                            "yhi": lax.rem(yh + dh, NYH),
                            "core": lax.rem(co + dc, NCO),
                        }

    partner = {"core": 1 - co}
    ypair = {"ylo": 1 - yl}

    local = [
        pltpu.make_async_copy(virt, VIRT.at[pl.ds(x * 1024, 1024)], lsem.at[0]),
        pltpu.make_async_copy(occ.at[pl.ds(a * 128, 128)], OCC.at[yl * 8 + z], lsem.at[1]),
        pltpu.make_async_copy(ints, AV, lsem.at[2]),
    ]
    for c in local:
        c.start()

    barrier = pltpu.get_barrier_semaphore()
    peers = [shift("row", NX, x, d) for d in range(1, NX)]
    peers += [shift("z", NZ, z, d) for d in range(1, NZ)]
    peers += list(ypeers())
    for p in peers:
        pl.semaphore_signal(barrier, inc=1, device_id=p, device_id_type=MESH)
    pl.semaphore_wait(barrier, len(peers))

    def vq(r, half, quarter):
        return VIRT.at[pl.ds(r * 1024 + half * 512 + quarter * 256, 256)]

    def own_vq(quarter):
        return virt.at[pl.ds(co * 512 + quarter * 256, 256)]

    def xblk(d):
        return lax.rem(x + d + NX, NX)

    def occ_rows(c, r0, n):
        return OCC.at[c, pl.ds(r0, n)]

    def own_occ(r0, n):
        return occ.at[pl.ds(a * 128 + r0, n)]

    def zat(d):
        return lax.rem(z + d + NZ, NZ)

    SIGN = {"+": 1, "-": -1}
    xs = {}
    for d, order in (("+", (0, 1)), ("-", (1, 0))):
        xs[d] = [
            send(own_vq(q), vq(x, co, q), **shift("row", NX, x, SIGN[d])) for q in order
        ]
    ya = send(own_occ(0, 64), occ_rows(yl * 8 + z, 0, 64), **ypair)
    za = {}
    for name, r0 in (("A", 0), ("B", 64)):
        for d in "+-":
            za[name, d, 1] = send(
                own_occ(r0, 64), occ_rows(yl * 8 + z, r0, 64), **shift("z", NZ, z, SIGN[d])
            )
    yb = [send(own_occ(64, 64), occ_rows(yl * 8 + z, 64, 64), **ypair)]

    lane = iota((8, 128), 1)
    subl = iota((8, 128), 0)
    idx = [listed[0, n] for n in range(8)]
    own = [lax.shift_right_logical(v, 3) for v in idx]
    pos = [jnp.bitwise_and(v, 7) for v in idx]
    rank = []
    for n in range(8):
        r = jnp.int32(0)
        for m in range(n):
            r = r + jnp.where(own[m] == own[n], 1, 0).astype(jnp.int32)
        rank.append(r)
    table = jnp.zeros((8, 128), F32)
    for n in range(8):
        hit = (subl == own[n]) & (lane // 4 == a * 2 + rank[n])
        table = table + jnp.where(hit, (pos[n] + 1).astype(F32), 0.0)
    LSRC[...] = table
    LB[a] = table
    lab = []
    for dh in range(NYH):
        for dc in range(NCO):
            if dh or dc:
                lab.append(
                    send(LSRC, LB.at[a], yhi=lax.rem(yh + dh, NYH), core=lax.rem(co + dc, NCO))
                )

    ya.wait_recv()
    for d in "+-":
        c = (1 - yl) * 8 + z
        za["P", d, 1] = send(occ_rows(c, 0, 64), occ_rows(c, 0, 64), **shift("z", NZ, z, SIGN[d]))

    def relay(name, d, step):
        s = SIGN[d]
        r0 = 64 if name == "B" else 0
        c = ((1 - yl) if name == "P" else yl) * 8 + zat(-s * step)
        za[name, d, step].wait_recv()
        if step <= 2:
            za[name, d, step + 1] = send(
                occ_rows(c, r0, 64), occ_rows(c, r0, 64), **shift("z", NZ, z, s)
            )
        elif step == 3:
            h0 = r0 + (0 if d == "+" else 32)
            za[name, d, 4] = send(
                occ_rows(c, h0, 32), occ_rows(c, h0, 32), **shift("z", NZ, z, s)
            )
        if name == "B" and step <= 3:
            yb.append(send(occ_rows(c, 64, 64), occ_rows(c, 64, 64), **ypair))

    def zstep(step):
        for name in ("A", "B", "P"):
            for d in "+-":
                relay(name, d, step)
        if step == 4:
            c = yl * 8 + zat(4)
            yb.append(send(occ_rows(c, 64, 64), occ_rows(c, 64, 64), **ypair))

    fwd = []

    def xfwd(r, q):
        fwd.append(send(vq(r, co, q), vq(r, co, q), **partner))

    zstep(1)
    for d, q in (("+", 0), ("-", 1)):
        s = SIGN[d]
        xs[d][0].wait_recv()
        r = xblk(-s)
        xs[d].append(send(vq(r, co, q), vq(r, co, q), **shift("row", NX, x, s)))
        xfwd(r, q)
    zstep(2)
    for d, q in (("+", 1), ("-", 0)):
        xs[d][1].wait_recv()
        xfwd(xblk(-SIGN[d]), q)
    zstep(3)
    for d, q in (("+", 0), ("-", 1)):
        xs[d][2].wait_recv()
        xfwd(xblk(2), q)
    zstep(4)
    for c in local:
        c.wait()
    for c in fwd:
        c.wait_recv()
    for c in yb:
        c.wait_recv()

    def mm(c, acc):
        return acc + jnp.dot(
            OCC[c], VIRT[pl.ds(pl.multiple_of(c * 256, 256), 256), :], preferred_element_type=F32
        )

    acc = lax.fori_loop(0, NYL * NZ, mm, jnp.zeros((128, 256), F32), unroll=4)
    for q in range(2):
        ROWS[q] = acc[:, q * 128 : (q + 1) * 128]
    tiles_from_rows(ROWS, FL)
    for m in range(32):
        TILES[a, :, m * 128 : (m + 1) * 128] = FL[m * 8 : (m + 1) * 8, :].astype(BF)

    def th(o, h):
        return TILES.at[o, :, pl.ds(h * 2048, 2048)]

    core_own = send(TILES.at[a], TILES.at[a], **partner)
    ts = {}
    for d, order in (("+", (0, 1)), ("-", (1, 0))):
        ts[d] = [send(th(a, h), th(a, h), **shift("yhi", NYH, yh, SIGN[d])) for h in order]
    tf = []

    def own_at(d):
        return lax.rem(yh + d + NYH, NYH) * 2 + co

    def tfwd(o, h):
        tf.append(send(th(o, h), th(o, h), **partner))

    for d, h in (("+", 0), ("-", 1)):
        s = SIGN[d]
        ts[d][0].wait_recv()
        o = own_at(-s)
        ts[d].append(send(th(o, h), th(o, h), **shift("yhi", NYH, yh, s)))
        tfwd(o, h)
    for d, h in (("+", 1), ("-", 0)):
        ts[d][1].wait_recv()
        tfwd(own_at(-SIGN[d]), h)
    for d, h in (("+", 0), ("-", 1)):
        ts[d][2].wait_recv()
        tfwd(own_at(2), h)
    core_own.wait_recv()
    for c in tf:
        c.wait_recv()

    for o in range(8):
        TF[o * 8 : (o + 1) * 8, :] = TILES[o].astype(F32)
    s64 = iota((8, 64), 1)
    n64 = iota((8, 64), 0)
    pick = jnp.zeros((8, 64), F32)
    for n in range(8):
        pick = pick + jnp.where((n64 == n) & (s64 == idx[n]), 1.0, 0.0)
    chosen = jnp.dot(pick.astype(BF), TF[...].astype(BF), preferred_element_type=F32)

    def contract(p, _):
        v = AV[p].astype(F32) * chosen
        s = v[:, 0:128]
        for m in range(1, 32):
            s = s + v[:, m * 128 : (m + 1) * 128]
        ACC[p] = s
        return 0

    lax.fori_loop(0, 32, contract, 0, unroll=2)
    part = jnp.sum(jnp.sum(ACC[...], axis=1), axis=1, keepdims=True)
    lane32 = iota((32, 128), 1)
    sub32 = iota((32, 128), 0)
    spread = jnp.where(lane32 == sub32 + lax.rem(a, 4) * 32, part, 0.0)
    spread = jnp.sum(spread, axis=0, keepdims=True)
    coeff = jnp.where(subl == a // 4, jnp.broadcast_to(spread, (8, 128)), 0.0)

    def exchange(k, value, buf, slot, targets, n, between=None):
        CSRC[k] = value
        buf[slot] = value
        cs = [send(CSRC.at[k], buf.at[slot], **t) for t in targets]
        if between is not None:
            between()
        for c in cs:
            c.wait_recv()
        total = buf[0]
        for i in range(1, n):
            total = total + buf[i]
        return total

    def write_product():
        def one(o, _):
            for m in range(32):
                FL[m * 8 : (m + 1) * 8, :] = TF[
                    pl.ds(pl.multiple_of(o * 8, 8), 8), m * 128 : (m + 1) * 128
                ]
            rows_from_tiles(FL, ROWS)
            for q in range(2):
                prod_out[pl.ds(pl.multiple_of(o * 128, 128), 128), q * 128 : (q + 1) * 128] = ROWS[
                    q
                ].astype(BF)
            return 0

        lax.fori_loop(0, 8, one, 0)

    coeff = exchange(
        0, coeff, CZ, z, [shift("z", NZ, z, d) for d in range(1, NZ)], NZ, write_product
    )
    coeff = exchange(1, coeff, CX, x, [shift("row", NX, x, d) for d in range(1, NX)], NX)
    coeff = exchange(2, coeff, CY, yl * 8 + a, list(ypeers()), 16)

    row = jnp.sum(jnp.where(subl == a // 4, coeff, 0.0), axis=0, keepdims=True)
    mine = jnp.zeros((1, 32), F32)
    for k in range(4):
        mine = mine + jnp.where(lax.rem(a, 4) == k, row[:, k * 32 : (k + 1) * 32], 0.0)
    coeff_out[...] = mine

    scr = metric[:, 0:128] * coeff[0:1, :] + metric[:, 128:256] * coeff[1:2, :]
    scr = jnp.sum(scr, axis=1, keepdims=True)
    SCB[...] = jnp.broadcast_to(scr, (32, 128))

    def weigh(p, accs):
        s = SCB[pl.ds(p, 1), :]
        v = AV[p].astype(F32)
        return tuple(accs[m] + v[:, m * 128 : (m + 1) * 128] * s for m in range(32))

    accs = lax.fori_loop(
        0, 32, weigh, tuple(jnp.zeros((8, 128), F32) for _ in range(32))
    )
    for m in range(32):
        BV[:, m * 128 : (m + 1) * 128] = accs[m]
    i64 = iota((64, 8), 0)
    n8 = iota((64, 8), 1)
    out = jnp.zeros((64, 1024), F32)
    for q in range(4):
        sel = jnp.zeros((64, 8), F32)
        for n in range(8):
            hit = (n8 == n) & (i64 == own[n] * 8 + rank[n] * 4 + q)
            sel = sel + jnp.where(hit, 1.0, 0.0)
        out = out + jnp.dot(
            sel.astype(BF), BV[:, q * 1024 : (q + 1) * 1024].astype(BF), preferred_element_type=F32
        )
    for o in range(8):
        SB[o] = out[o * 8 : (o + 1) * 8, :].astype(BF)
    keep = pltpu.make_async_copy(SB.at[a], RB.at[a], lsem.at[3])
    keep.start()
    ex = []
    for dh in range(NYH):
        for dc in range(NCO):
            if dh or dc:
                h2 = lax.rem(yh + dh, NYH)
                c2 = lax.rem(co + dc, NCO)
                ex.append(send(SB.at[h2 * 2 + c2], RB.at[a], yhi=h2, core=c2))
    for c in lab:
        c.wait_recv()
    labels = LB[0]
    for o in range(1, 8):
        labels = labels + LB[o]
    labels = jnp.sum(jnp.where(subl == a, labels, 0.0), axis=0, keepdims=True)[:, 0:64]
    t64 = iota((8, 64), 0).astype(F32)
    q64 = jnp.bitwise_and(iota((8, 64), 1), 3)
    keep.wait()
    for c in ex:
        c.wait_recv()
    arrived = jnp.concatenate([RB[o].astype(F32) for o in range(8)], axis=0).astype(BF)
    for q in range(4):
        place = jnp.where((labels == t64 + 1.0) & (q64 == q), 1.0, 0.0).astype(BF)
        d = jnp.dot(place, arrived, preferred_element_type=F32)
        for m in range(8):
            FL[(q * 8 + m) * 8 : (q * 8 + m + 1) * 8, :] = d[:, m * 128 : (m + 1) * 128]
    rows_from_tiles(FL, ROWS)
    deriv = jnp.concatenate([ROWS[0], ROWS[1]], axis=1).astype(BF)

    def partial(i, _):
        FP[i] = lax.dot_general(
            VIRT[pl.ds(pl.multiple_of(i * 256, 256), 256), :], deriv,
            (((1,), (1,)), ((), ())), preferred_element_type=F32,
        )
        return 0

    lax.fori_loop(0, 16, partial, 0, unroll=2)

    mycol = yl * 8
    other = (1 - yl) * 8
    order = [4, 3, -3, 2, -2, 1, -1, 0]
    ys = {}
    for k, d in enumerate(order):
        SY[k] = FP[other + zat(d), 128:256, :].astype(BF)
        ys[d] = send(SY.at[k], RY.at[k], **ypair)
    ys[-4] = ys[4]
    YI = {d: k for k, d in enumerate(order)}
    items = {"A": (mycol, 0), "P": (other, 0), "B": (mycol, 128)}
    IX = {"A": 0, "P": 1, "B": 2}
    DX = {"+": 0, "-": 1}
    rs = {}
    added = set()

    def ring(name, d, step):
        base, r0 = items[name]
        i, j, s = IX[name], DX[d], SIGN[d]
        dist = s * (5 - step)
        dest = zat(dist)
        if step > 1:
            rs[name, d, step - 1].wait_recv()
        if name == "B":
            key = 4 if abs(dist) == 4 else dist
            if key not in added:
                added.add(key)
                ys[key].wait_recv()
        extra = YI[4 if abs(dist) == 4 else dist]
        to = shift("z", NZ, z, s)
        if step == 1:
            h0 = 0 if d == "+" else 64
            v = FP[base + dest, r0 + h0 : r0 + h0 + 64, :]
            if name == "B":
                v = v + RY[extra, h0 : h0 + 64, :].astype(F32)
            SH[i, j] = v.astype(BF)
            rs[name, d, 1] = send(SH.at[i, j], RH.at[i, j], **to)
            return
        v = FP[base + dest, r0 : r0 + 128, :]
        if name == "B":
            v = v + RY[extra].astype(F32)
        if step == 2:
            h0 = 0 if d == "+" else 64
            got = RH[i, j].astype(F32)
            zero = jnp.zeros((64, 128), F32)
            v = v + jnp.concatenate([got, zero] if d == "+" else [zero, got], axis=0)
        else:
            v = v + RF[i, j, step - 3].astype(F32)
        SF[i, j, step - 2] = v.astype(BF)
        rs[name, d, step] = send(SF.at[i, j, step - 2], RF.at[i, j, step - 2], **to)

    for step in range(1, 5):
        for name in ("P", "A", "B"):
            for d in "+-":
                ring(name, d, step)

    def final(name):
        base, r0 = items[name]
        i = IX[name]
        v = FP[base + z, r0 : r0 + 128, :]
        for d in "+-":
            rs[name, d, 4].wait_recv()
            v = v + RF[i, DX[d], 2].astype(F32)
        return v

    SP[...] = final("P").astype(BF)
    yp = send(SP, RP, **ypair)
    va = final("A")
    ys[0].wait_recv()
    force_out[128:256, :] = final("B") + RY[YI[0]].astype(F32)
    yp.wait_recv()
    force_out[0:128, :] = va + RP[...].astype(F32)
    for c in started:
        c.wait_send()
    assert count[0] <= NCOPY


def on_device(green_occ, green_virt, integrals, listed, metric):
    vm = pltpu.VMEM
    hbm = pl.BlockSpec(memory_space=pl.ANY)
    inv = pl.BlockSpec(memory_space=pltpu.VMEM)
    product, coeff, force = pl.pallas_call(
        body,
        out_shape=(
            jax.ShapeDtypeStruct((1024, 256), BF),
            jax.ShapeDtypeStruct((1, 32), F32),
            jax.ShapeDtypeStruct((256, 128), F32),
        ),
        in_specs=[pl.BlockSpec(memory_space=pltpu.SMEM), hbm, hbm, hbm, inv],
        out_specs=(inv, inv, inv),
        scratch_shapes=[
            vm((4096, 256), BF),
            vm((16, 128, 256), BF),
            vm((32, 8, 4096), BF),
            vm((256, 128), F32),
            vm((2, 128, 128), F32),
            vm((8, 8, 4096), BF),
            vm((64, 4096), F32),
            vm((3, 8, 128), F32),
            vm((8, 8, 128), F32),
            vm((4, 8, 128), F32),
            vm((16, 8, 128), F32),
            vm((32, 8, 128), F32),
            vm((32, 128), F32),
            vm((8, 128), F32),
            vm((8, 8, 128), F32),
            vm((8, 4096), F32),
            vm((8, 8, 1024), BF),
            vm((8, 8, 1024), BF),
            vm((16, 256, 128), F32),
            vm((3, 2, 64, 128), BF),
            vm((3, 2, 64, 128), BF),
            vm((3, 2, 3, 128, 128), BF),
            vm((3, 2, 3, 128, 128), BF),
            vm((8, 128, 128), BF),
            vm((8, 128, 128), BF),
            vm((128, 128), BF),
            vm((128, 128), BF),
            pltpu.SemaphoreType.DMA((NCOPY,)),
            pltpu.SemaphoreType.DMA((NCOPY,)),
            pltpu.SemaphoreType.DMA((4,)),
        ],
        compiler_params=pltpu.CompilerParams(
            collective_id=0, has_side_effects=True, vmem_limit_bytes=40 << 20
        ),
        name="force_window",
    )(
        listed.reshape(1, 8), green_occ, green_virt, integrals.reshape(32, 8, 4096), metric
    )
    return product, coeff.reshape(32), force


def solution(mesh):
    split = Mesh(
        mesh.devices.reshape(NX, NYL, NZ, NYH, NCO), ("row", "ylo", "z", "yhi", "core")
    )
    col, aux = ("ylo", "z"), ("yhi", "core")
    return jax.shard_map(
        on_device,
        mesh=split,
        in_specs=(
            P("row", col),
            P("row", col),
            P("row", col, aux, None, None),
            P("row", col, aux, None),
            P(aux, None),
        ),
        out_specs=(P("row", col), P(aux), P(col, ("row", *aux))),
        check_vma=False,
    )
```

time: 223 us -> 93.5 us (0.42)
  Pallas kernels: 0 us -> 85.5 us
  waiting for transfers between devices: 84.4 us -> 0 us
  blocking collectives: 80.9 us -> 0 us
  starting transfers between devices: 15.7 us -> 0 us
  between operations: 14.2 us -> 0.65 us
  matrix products: 12.6 us -> 0 us
  local copies, waits for them, and re-layouts: 12.3 us -> 7.04 us
  other arithmetic: 2.33 us -> 0 us
    pallas_call x0 -> x1, Pallas kernels: none -> 85.5 us  [on_device(): pl.pallas_call(body, out_shape=(jax.ShapeDtypeStruct((1024, 256), BF), ja...]
    all_to_all x3 -> x0, waiting for transfers between devices: 79.2 us -> none  [the longest x1 48.5 us: sent_and_summed(): lax.all_to_all(pieces, axis, split_axis=0, concat_axis=0, tiled=True)]
    psum x5 -> x0, blocking collectives: 43.2 us -> none  [over_axes(): x = lax.psum(x, axis)]
    all_to_all x1 -> x0, blocking collectives: 37.7 us -> none  [from_everyone(): lax.all_to_all(jnp.broadcast_to(x[None], (count, *x.shape)), axis, 0, 0,...]
    all_to_all x3 -> x0, starting transfers between devices: 15.7 us -> none  [the longest x1 5.84 us: from_everyone(): lax.all_to_all(jnp.broadcast_to(x[None], (count, *x.shape)), axis, 0, 0,...]
    dot_general x9 -> x0, matrix products: 12.6 us -> none  [the longest x1 4.25 us: on_device(): lax.dot_general(local_ints, chosen, (((1, 2), (0, 1)), ((), ())), preferr...]
    unnamed x11 -> x13, local copies, waits for them, and re-layouts: 1.07 us -> 7.04 us
    all_gather x1 -> x0, waiting for transfers between devices: 4.5 us -> none  [on_device(): virtual = lax.all_gather(green_virt, 'row', axis=0, tiled=True)]
  transfers between devices with their start and end apart: 4 -> 0, of which waited for: 4 -> 0; matrix products, arithmetic and copies ran while one was open for 1% -> 0% of each run, Pallas kernels for 0% -> 0%
where the time goes in v1:
time: 93.5 us; the launch traced here: 93.2 us
  Pallas kernels  85.5 us (91%)
  local copies, waits for them, and re-layouts  7.04 us (8%)
    pallas_call x1, Pallas kernels, on_device(): pl.pallas_call(body, out_shape=(jax.ShapeDtypeStruct((1024, 256), BF), ja...  85.5 us
    unnamed x13, local copies, waits for them, and re-layouts  7.04 us

profile of v1, /device:TPU:8, one launch (start us, length us, event | category | flops | bytes accessed | tf_op | source)
XLA Modules:
  0.0 93.2 jit_solution(2360944330499227273)
XLA Ops:
  0.6 0.0 copy-start
  0.6 1.6 %copy-done = bf16[1,1,32,8,4096]{4,3,2,1,0:T(8,128)(2,1)S(1)} copy-done((bf16[1,1,32,8,4096]{4,3,2,1,0:T(8,128)(2,1)S(1)}, bf16[1,1,32,8,4096]{4,3,2,1,0:T(8,128)(2,1)}, u32[]{:S(2)}) %copy-start) | copy-done | bytes 2097176
  2.2 0.0 copy-start.1
  2.2 1.0 %copy-done.1 = bf16[1024,256]{1,0:T(8,128)(2,1)S(1)} copy-done((bf16[1024,256]{1,0:T(8,128)(2,1)S(1)}, bf16[1024,256]{1,0:T(8,128)(2,1)}, u32[]{:S(2)}) %copy-start.1) | copy-done | bytes 524312
  3.3 0.0 copy-start.2
  3.3 1.0 %copy-done.2 = bf16[1024,256]{1,0:T(8,128)(2,1)S(1)} copy-done((bf16[1024,256]{1,0:T(8,128)(2,1)S(1)}, bf16[1024,256]{1,0:T(8,128)(2,1)}, u32[]{:S(2)}) %copy-start.2) | copy-done | bytes 524312
  4.3 0.0 copy-start.3
  4.3 0.8 copy-done.3
  5.1 0.0 copy-start.4
  5.1 0.7 copy-done.4
  5.7 85.5 %force_window.1 = (bf16[1024,256]{1,0:T(8,128)(2,1)S(1)}, f32[1,32]{1,0:T(1,128)S(1)}, f32[256,128]{1,0:T(8,128)S(1)}) custom-call(s32[1,8]{1,0:T(1,128)S(1)} %bitcast.4, bf16[1024,256]{1,0:T(8,128)(2,1)S(1)} %copy-done.1, bf16[1024,256]{1,0:T(8,128)(2,1)S(1)} %copy-done.2, bf16[32,8,4096]{2,1,0:T(8,128)(2,1)S(1)} %bitcast.3, f32[32,256]{1,0:T(8,128)S(1)} %copy-done.3), custom_call_target="tpu_custom_call" | custom-call | tf_op jit(solution)/shard_map/force_window/pallas_call | solution.py:471
  91.2 0.8 copy.11
  92.0 0.5 copy.12
  92.5 0.7 copy.13
Async XLA Ops:
  0.6 1.6 %copy-start = (bf16[1,1,32,8,4096]{4,3,2,1,0:T(8,128)(2,1)S(1)}, bf16[1,1,32,8,4096]{4,3,2,1,0:T(8,128)(2,1)}, u32[]{:S(2)}) copy-start(bf16[1,1,32,8,4096]{4,3,2,1,0:T(8,128)(2,1)} %param.7) | copy-start | bytes 6291460
  2.2 1.0 %copy-start.1 = (bf16[1024,256]{1,0:T(8,128)(2,1)S(1)}, bf16[1024,256]{1,0:T(8,128)(2,1)}, u32[]{:S(2)}) copy-start(bf16[1024,256]{1,0:T(8,128)(2,1)} %occ.1) | copy-start | bytes 1572868
  3.3 1.0 %copy-start.2 = (bf16[1024,256]{1,0:T(8,128)(2,1)S(1)}, bf16[1024,256]{1,0:T(8,128)(2,1)}, u32[]{:S(2)}) copy-start(bf16[1024,256]{1,0:T(8,128)(2,1)} %virt.1) | copy-start | bytes 1572868
  4.3 0.8 copy-start.3
  5.1 0.7 copy-start.4

commit v2 on v1

v2 whole, which is shorter than its diff:
```python
import jax
import jax.numpy as jnp
from jax import lax
from jax.experimental import pallas as pl
from jax.experimental.pallas import tpu as pltpu
from jax.sharding import Mesh
from jax.sharding import PartitionSpec as P

MESH = pl.DeviceIdType.MESH
BF = jnp.bfloat16
F32 = jnp.float32
NX, NYL, NZ, NYH, NCO = 4, 2, 8, 4, 2
NCOPY = 160


def iota(shape, dim):
    return lax.broadcasted_iota(jnp.int32, shape, dim)


def rows_from_tiles(fl, rows):
    left = iota((32, 128), 1) < 64
    for br in range(2):
        for q in range(2):
            t = br * 4 + 2 * q
            a = fl[pl.ds(t, 32, stride=8), :]
            b = fl[pl.ds(t + 1, 32, stride=8), :]
            even = jnp.where(left, a, pltpu.roll(b, 64, 1))
            odd = jnp.where(left, pltpu.roll(a, 64, 1), b)
            rows[q, pl.ds(br * 64, 32, stride=2), :] = even
            rows[q, pl.ds(br * 64 + 1, 32, stride=2), :] = odd


def tiles_from_rows(rows, fl):
    left = iota((32, 128), 1) < 64
    for br in range(2):
        for q in range(2):
            t = br * 4 + 2 * q
            even = rows[q, pl.ds(br * 64, 32, stride=2), :]
            odd = rows[q, pl.ds(br * 64 + 1, 32, stride=2), :]
            fl[pl.ds(t, 32, stride=8), :] = jnp.where(left, even, pltpu.roll(odd, 64, 1))
            fl[pl.ds(t + 1, 32, stride=8), :] = jnp.where(left, pltpu.roll(even, 64, 1), odd)


def body(
    listed, occ, virt, ints, metric, prod_out, coeff_out, force_out,
    VIRT, OCC, AV, FL, ROWS, PR, CSRC, CZX, CY, ACC, SCB, LSRC, LB,
    BV, SB, RB, ST, RT, FP, S4, R4, S3, R3, S2, R2, S1, R1, SY, RY, ssem, rsem, lsem,
):
    x = lax.axis_index("row")
    yl = lax.axis_index("ylo")
    z = lax.axis_index("z")
    yh = lax.axis_index("yhi")
    co = lax.axis_index("core")
    a = yh * 2 + co
    count = [0]
    started = []

    def send(src, dst, **to):
        k = count[0]
        count[0] += 1
        c = pltpu.make_async_remote_copy(
            src_ref=src, dst_ref=dst, send_sem=ssem.at[k], recv_sem=rsem.at[k],
            device_id=to, device_id_type=MESH,
        )
        c.start()
        started.append(c)
        return c

    def shift(axis, n, me, d):
        return {axis: lax.rem(me + d + n, n)}

    def ypeers():
        for dl in range(NYL):
            for dh in range(NYH):
                for dc in range(NCO):
                    if dl or dh or dc:
                        yield {
                            "ylo": lax.rem(yl + dl, NYL),
                            "yhi": lax.rem(yh + dh, NYH),
                            "core": lax.rem(co + dc, NCO),
                        }

    partner = {"core": 1 - co}
    ypair = {"ylo": 1 - yl}

    local = [
        pltpu.make_async_copy(virt, VIRT.at[pl.ds(x * 1024, 1024)], lsem.at[0]),
        pltpu.make_async_copy(occ.at[pl.ds(a * 128, 128)], OCC.at[yl * 8 + z], lsem.at[1]),
        pltpu.make_async_copy(ints, AV, lsem.at[2]),
    ]
    for c in local:
        c.start()

    barrier = pltpu.get_barrier_semaphore()
    zx = [
        {"row": lax.rem(x + dx, NX), "z": lax.rem(z + dz, NZ)}
        for dx in range(NX) for dz in range(NZ) if dx or dz
    ]
    diag = [{"ylo": 1 - yl, "z": lax.rem(z + d + NZ, NZ)} for d in (1, -1)]
    peers = zx + diag + list(ypeers())
    for p in peers:
        pl.semaphore_signal(barrier, inc=1, device_id=p, device_id_type=MESH)
    pl.semaphore_wait(barrier, len(peers))

    def vq(r, half, quarter):
        return VIRT.at[pl.ds(r * 1024 + half * 512 + quarter * 256, 256)]

    def own_vq(quarter):
        return virt.at[pl.ds(co * 512 + quarter * 256, 256)]

    def xblk(d):
        return lax.rem(x + d + NX, NX)

    def occ_half(c, h):
        return OCC.at[c, pl.ds(h * 64, 64)]

    def own_half(h):
        return occ.at[pl.ds(a * 128 + h * 64, 64)]

    def zat(d):
        return lax.rem(z + d + NZ, NZ)

    SIGN = {"+": 1, "-": -1}
    xs = {}
    for d, order in (("+", (0, 1)), ("-", (1, 0))):
        xs[d] = [
            send(own_vq(q), vq(x, co, q), **shift("row", NX, x, SIGN[d])) for q in order
        ]
    cme = yl * 8 + z
    base = {"O": yl * 8, "P": (1 - yl) * 8}
    order = {"+": (0, 1), "-": (1, 0)}
    zs = {}
    zy = []
    for k in range(2):
        for L in "OP":
            for d in "+-":
                h = order[d][k]
                to = shift("z", NZ, z, SIGN[d])
                if L == "P":
                    to["ylo"] = 1 - yl
                zs[L, d, 1, h] = send(own_half(h), occ_half(cme, h), **to)
        zy.append(send(own_half(k), occ_half(cme, k), **ypair))

    lane = iota((8, 128), 1)
    subl = iota((8, 128), 0)
    idx = [listed[0, n] for n in range(8)]
    own = [lax.shift_right_logical(v, 3) for v in idx]
    pos = [jnp.bitwise_and(v, 7) for v in idx]
    rank = []
    for n in range(8):
        r = jnp.int32(0)
        for m in range(n):
            r = r + jnp.where(own[m] == own[n], 1, 0).astype(jnp.int32)
        rank.append(r)
    table = jnp.zeros((8, 128), F32)
    for n in range(8):
        hit = (subl == own[n]) & (lane // 4 == a * 2 + rank[n])
        table = table + jnp.where(hit, (pos[n] + 1).astype(F32), 0.0)
    LSRC[...] = table
    LB[a] = table
    lab = []
    for dh in range(NYH):
        for dc in range(NCO):
            if dh or dc:
                lab.append(
                    send(LSRC, LB.at[a], yhi=lax.rem(yh + dh, NYH), core=lax.rem(co + dc, NCO))
                )

    def relay(step):
        for k in range(2):
            for L in "OP":
                for d in "+-":
                    s = SIGN[d]
                    h = order[d][k]
                    zs[L, d, step, h].wait_recv()
                    blk = occ_half(base[L] + zat(-s * step), h)
                    if step <= 2:
                        zs[L, d, step + 1, h] = send(blk, blk, **shift("z", NZ, z, s))
                    if step == 2 and k == 0:
                        zs[L, d, 4, h] = send(blk, blk, **shift("z", NZ, z, 2 * s))

    fwd = []

    def xfwd(r, q):
        fwd.append(send(vq(r, co, q), vq(r, co, q), **partner))

    relay(1)
    for d, q in (("+", 0), ("-", 1)):
        s = SIGN[d]
        xs[d][0].wait_recv()
        r = xblk(-s)
        xs[d].append(send(vq(r, co, q), vq(r, co, q), **shift("row", NX, x, s)))
        xfwd(r, q)
    relay(2)
    for d, q in (("+", 1), ("-", 0)):
        xs[d][1].wait_recv()
        xfwd(xblk(-SIGN[d]), q)
    for d, q in (("+", 0), ("-", 1)):
        xs[d][2].wait_recv()
        xfwd(xblk(2), q)
    for c in local[:2]:
        c.wait()
    for c in zy:
        c.wait_recv()
    for c in lab:
        c.wait_recv()
    for c in fwd:
        c.wait_recv()

    def mm(c, acc):
        return acc + jnp.dot(
            OCC[c], VIRT[pl.ds(pl.multiple_of(c * 256, 256), 256), :], preferred_element_type=F32
        )

    acc = jnp.zeros((128, 256), F32)
    for dist in (0, 1, -1, 2, -2):
        for L in "OP":
            acc = mm(base[L] + zat(dist), acc)
    relay(3)
    for dist in (3, -3):
        for L in "OP":
            acc = mm(base[L] + zat(dist), acc)
    for L in "OP":
        for d in "+-":
            zs[L, d, 4, order[d][0]].wait_recv()
        acc = mm(base[L] + zat(4), acc)
    PR[...] = acc.astype(BF)
    for q in range(2):
        ROWS[q] = acc[:, q * 128 : (q + 1) * 128]
    tiles_from_rows(ROWS, FL)
    for m in range(32):
        BV[:, m * 128 : (m + 1) * 128] = FL[m * 8 : (m + 1) * 8, :]

    labels = LB[0]
    for o in range(1, 8):
        labels = labels + LB[o]
    labels = jnp.sum(jnp.where(subl == a, labels, 0.0), axis=0, keepdims=True)[:, 0:64]
    square = jnp.broadcast_to(labels, (64, 64))
    labels_down = jnp.sum(
        jnp.where(iota((64, 64), 0) == iota((64, 64), 1), square, 0.0), axis=1, keepdims=True
    )
    i64 = iota((64, 8), 0)
    n8 = iota((64, 8), 1)
    q64 = jnp.bitwise_and(i64, 3)
    out = jnp.zeros((64, 1024), F32)
    for q in range(4):
        take = jnp.where((labels_down == (n8 + 1).astype(F32)) & (q64 == q), 1.0, 0.0)
        out = out + jnp.dot(
            take.astype(BF), BV[:, q * 1024 : (q + 1) * 1024].astype(BF), preferred_element_type=F32
        )
    for o in range(8):
        ST[o] = out[o * 8 : (o + 1) * 8, :].astype(BF)

    def to_owners(src, dst, sem):
        keep = pltpu.make_async_copy(src.at[a], dst.at[a], sem)
        keep.start()
        cs = []
        for dh in (2, 1, 3, 0):
            for dc in range(NCO):
                if dh or dc:
                    h2 = lax.rem(yh + dh, NYH)
                    c2 = lax.rem(co + dc, NCO)
                    cs.append(send(src.at[h2 * 2 + c2], dst.at[a], yhi=h2, core=c2))
        return keep, cs

    keep, cs = to_owners(ST, RT, lsem.at[3])
    keep.wait()
    for c in cs:
        c.wait_recv()

    def prow(o):
        return prod_out.at[pl.ds(o * 128, 128)]

    pown = pltpu.make_async_copy(PR, prow(a), lsem.at[4])
    pown.start()
    pcore = send(PR, prow(a), **partner)
    pfar = [send(PR, prow(a), **shift("yhi", NYH, yh, d)) for d in (1, 3, 2)]

    arrived = jnp.concatenate([RT[o].astype(F32) for o in range(8)], axis=0).astype(BF)
    s64 = iota((8, 64), 1)
    n64 = iota((8, 64), 0)
    chosen = []
    for q in range(4):
        pick = jnp.zeros((8, 64), F32)
        for n in range(8):
            hit = (n64 == n) & (s64 == own[n] * 8 + rank[n] * 4 + q)
            pick = pick + jnp.where(hit, 1.0, 0.0)
        chosen.append(jnp.dot(pick.astype(BF), arrived, preferred_element_type=F32))
    chosen = jnp.concatenate(chosen, axis=1)
    local[2].wait()

    def contract(p, _):
        v = AV[p].astype(F32) * chosen
        s = v[:, 0:128]
        for m in range(1, 32):
            s = s + v[:, m * 128 : (m + 1) * 128]
        ACC[p] = s
        return 0

    lax.fori_loop(0, 32, contract, 0, unroll=2)
    part = jnp.sum(jnp.sum(ACC[...], axis=1), axis=1, keepdims=True)
    lane32 = iota((32, 128), 1)
    sub32 = iota((32, 128), 0)
    spread = jnp.where(lane32 == sub32 + lax.rem(a, 4) * 32, part, 0.0)
    spread = jnp.sum(spread, axis=0, keepdims=True)
    coeff = jnp.where(subl == a // 4, jnp.broadcast_to(spread, (8, 128)), 0.0)

    def exchange(k, value, buf, slot, targets, n):
        CSRC[k] = value
        buf[slot] = value
        cs = [send(CSRC.at[k], buf.at[slot], **t) for t in targets]
        for c in cs:
            c.wait_recv()
        total = buf[0]
        for i in range(1, n):
            total = total + buf[i]
        return total

    coeff = exchange(0, coeff, CZX, x * 8 + z, zx, NX * NZ)
    pfwd = []
    for c, d in zip(pfar, (1, 3, 2)):
        c.wait_recv()
        o = lax.rem(yh + NYH - d, NYH) * 2 + co
        pfwd.append(send(prow(o), prow(o), **partner))
    coeff = exchange(1, coeff, CY, yl * 8 + a, list(ypeers()), 16)

    row = jnp.sum(jnp.where(subl == a // 4, coeff, 0.0), axis=0, keepdims=True)
    mine = jnp.zeros((1, 32), F32)
    for k in range(4):
        mine = mine + jnp.where(lax.rem(a, 4) == k, row[:, k * 32 : (k + 1) * 32], 0.0)
    coeff_out[...] = mine

    scr = metric[:, 0:128] * coeff[0:1, :] + metric[:, 128:256] * coeff[1:2, :]
    scr = jnp.sum(scr, axis=1, keepdims=True)
    SCB[...] = jnp.broadcast_to(scr, (32, 128))

    def weigh(p, accs):
        s = SCB[pl.ds(p, 1), :]
        v = AV[p].astype(F32)
        return tuple(accs[m] + v[:, m * 128 : (m + 1) * 128] * s for m in range(32))

    accs = lax.fori_loop(
        0, 32, weigh, tuple(jnp.zeros((8, 128), F32) for _ in range(32))
    )
    for m in range(32):
        BV[:, m * 128 : (m + 1) * 128] = accs[m]
    out = jnp.zeros((64, 1024), F32)
    for q in range(4):
        sel = jnp.zeros((64, 8), F32)
        for n in range(8):
            hit = (n8 == n) & (i64 == own[n] * 8 + rank[n] * 4 + q)
            sel = sel + jnp.where(hit, 1.0, 0.0)
        out = out + jnp.dot(
            sel.astype(BF), BV[:, q * 1024 : (q + 1) * 1024].astype(BF), preferred_element_type=F32
        )
    for o in range(8):
        SB[o] = out[o * 8 : (o + 1) * 8, :].astype(BF)
    keep, cs = to_owners(SB, RB, lsem.at[3])
    t64 = iota((8, 64), 0).astype(F32)
    l64 = jnp.bitwise_and(iota((8, 64), 1), 3)
    keep.wait()
    for c in cs:
        c.wait_recv()
    arrived = jnp.concatenate([RB[o].astype(F32) for o in range(8)], axis=0).astype(BF)
    for q in range(4):
        place = jnp.where((labels == t64 + 1.0) & (l64 == q), 1.0, 0.0).astype(BF)
        d = jnp.dot(place, arrived, preferred_element_type=F32)
        for m in range(8):
            FL[(q * 8 + m) * 8 : (q * 8 + m + 1) * 8, :] = d[:, m * 128 : (m + 1) * 128]
    rows_from_tiles(FL, ROWS)
    deriv = jnp.concatenate([ROWS[0], ROWS[1]], axis=1).astype(BF)

    def partial(i):
        return lax.dot_general(
            VIRT[pl.ds(pl.multiple_of(i * 256, 256), 256), :], deriv,
            (((1,), (1,)), ((), ())), preferred_element_type=F32,
        )

    IL = {"O": 0, "P": 1}
    ID = {"+": 0, "-": 1}
    fs = {}
    for L in "OP":
        v = partial(base[L] + zat(4))
        for d in "+-":
            h = order[d][0]
            i, j = IL[L], ID[d]
            S4[i, j] = v[h * 128 : (h + 1) * 128].astype(BF)
            fs[L, d, 4] = send(S4.at[i, j], R4.at[i, j], **shift("z", NZ, z, 2 * SIGN[d]))
    for L in "OP":
        for d in "+-":
            i, j = IL[L], ID[d]
            v = partial(base[L] + zat(3 * SIGN[d]))
            for h in order[d]:
                S3[i, j, h] = v[h * 128 : (h + 1) * 128].astype(BF)
                fs[L, d, 3, h] = send(
                    S3.at[i, j, h], R3.at[i, j, h], **shift("z", NZ, z, SIGN[d])
                )
    for dist in (2, -2, 1, -1, 0):
        for L in "OP":
            FP[base[L] + zat(dist)] = partial(base[L] + zat(dist))
    fy = []
    for h in range(2):
        SY[h] = FP[base["P"] + z, h * 128 : (h + 1) * 128, :].astype(BF)
        fy.append(send(SY.at[h], RY.at[h], **ypair))

    for k in (1, 0):
        for L in "OP":
            for d in "+-":
                i, j, s = IL[L], ID[d], SIGN[d]
                h = order[d][k]
                v = FP[base[L] + zat(2 * s), h * 128 : (h + 1) * 128, :]
                fs[L, d, 3, h].wait_recv()
                v = v + R3[i, j, h].astype(F32)
                if k == 0:
                    fs[L, d, 4].wait_recv()
                    v = v + R4[i, j].astype(F32)
                S2[i, j, h] = v.astype(BF)
                fs[L, d, 2, h] = send(S2.at[i, j, h], R2.at[i, j, h], **shift("z", NZ, z, s))
    for k in (1, 0):
        for L in "OP":
            for d in "+-":
                i, j, s = IL[L], ID[d], SIGN[d]
                h = order[d][k]
                v = FP[base[L] + zat(s), h * 128 : (h + 1) * 128, :]
                fs[L, d, 2, h].wait_recv()
                v = v + R2[i, j, h].astype(F32)
                S1[i, j, h] = v.astype(BF)
                to = shift("z", NZ, z, s)
                if L == "P":
                    to["ylo"] = 1 - yl
                fs[L, d, 1, h] = send(S1.at[i, j, h], R1.at[i, j, h], **to)
    pown.wait()
    pcore.wait_recv()
    for c in pfwd:
        c.wait_recv()
    for h in range(2):
        fy[h].wait_recv()
        v = FP[base["O"] + z, h * 128 : (h + 1) * 128, :] + RY[h].astype(F32)
        for L in "OP":
            for d in "+-":
                fs[L, d, 1, h].wait_recv()
                v = v + R1[IL[L], ID[d], h].astype(F32)
        force_out[h * 128 : (h + 1) * 128, :] = v
    for c in started:
        c.wait_send()
    assert count[0] <= NCOPY


def on_device(green_occ, green_virt, integrals, listed, metric):
    vm = pltpu.VMEM
    hbm = pl.BlockSpec(memory_space=pl.ANY)
    inv = pl.BlockSpec(memory_space=pltpu.VMEM)
    product, coeff, force = pl.pallas_call(
        body,
        out_shape=(
            jax.ShapeDtypeStruct((1024, 256), BF),
            jax.ShapeDtypeStruct((1, 32), F32),
            jax.ShapeDtypeStruct((256, 128), F32),
        ),
        in_specs=[pl.BlockSpec(memory_space=pltpu.SMEM), hbm, hbm, hbm, inv],
        out_specs=(hbm, inv, inv),
        scratch_shapes=[
            vm((4096, 256), BF),
            vm((16, 128, 256), BF),
            vm((32, 8, 4096), BF),
            vm((256, 128), F32),
            vm((2, 128, 128), F32),
            vm((128, 256), BF),
            vm((2, 8, 128), F32),
            vm((32, 8, 128), F32),
            vm((16, 8, 128), F32),
            vm((32, 8, 128), F32),
            vm((32, 128), F32),
            vm((8, 128), F32),
            vm((8, 8, 128), F32),
            vm((8, 4096), F32),
            vm((8, 8, 1024), BF),
            vm((8, 8, 1024), BF),
            vm((8, 8, 1024), BF),
            vm((8, 8, 1024), BF),
            vm((16, 256, 128), F32),
            vm((2, 2, 128, 128), BF),
            vm((2, 2, 128, 128), BF),
            vm((2, 2, 2, 128, 128), BF),
            vm((2, 2, 2, 128, 128), BF),
            vm((2, 2, 2, 128, 128), BF),
            vm((2, 2, 2, 128, 128), BF),
            vm((2, 2, 2, 128, 128), BF),
            vm((2, 2, 2, 128, 128), BF),
            vm((2, 128, 128), BF),
            vm((2, 128, 128), BF),
            pltpu.SemaphoreType.DMA((NCOPY,)),
            pltpu.SemaphoreType.DMA((NCOPY,)),
            pltpu.SemaphoreType.DMA((5,)),
        ],
        compiler_params=pltpu.CompilerParams(
            collective_id=0, has_side_effects=True, vmem_limit_bytes=60 << 20
        ),
        name="force_window",
    )(
        listed.reshape(1, 8), green_occ, green_virt, integrals.reshape(32, 8, 4096), metric
    )
    return product, coeff.reshape(32), force


def solution(mesh):
    split = Mesh(
        mesh.devices.reshape(NX, NYL, NZ, NYH, NCO), ("row", "ylo", "z", "yhi", "core")
    )
    col, aux = ("ylo", "z"), ("yhi", "core")
    return jax.shard_map(
        on_device,
        mesh=split,
        in_specs=(
            P("row", col),
            P("row", col),
            P("row", col, aux, None, None),
            P("row", col, aux, None),
            P(aux, None),
        ),
        out_specs=(P("row", col), P(aux), P(col, ("row", *aux))),
        check_vma=False,
    )
```

time: 93.5 us -> 83.8 us (0.90)
  the two profiles are of different devices: /device:TPU:8 before, /device:TPU:2 now
where the time goes in v2:
time: 83.8 us; the launch traced here: 83.5 us
  Pallas kernels  78.3 us (93%)
  local copies, waits for them, and re-layouts  4.6 us (5%)
    pallas_call x1, Pallas kernels, on_device(): pl.pallas_call(body, out_shape=(jax.ShapeDtypeStruct((1024, 256), BF), ja...  78.3 us
    unnamed x3, local copies, waits for them, and re-layouts  4.6 us

profile of v2, /device:TPU:2, one launch (start us, length us, event | category | flops | bytes accessed | tf_op | source)
XLA Modules:
  0.0 83.5 jit_solution(7467305605264095696)
XLA Ops:
  0.6 78.3 %force_window.1 = (bf16[1024,256]{1,0:T(8,128)(2,1)}, f32[1,32]{1,0:T(1,128)}, f32[256,128]{1,0:T(8,128)}) custom-call(s32[1,8]{1,0:T(1,128)} %bitcast.4, bf16[1024,256]{1,0:T(8,128)(2,1)} %occ.1, bf16[1024,256]{1,0:T(8,128)(2,1)} %virt.1, bf16[32,8,4096]{2,1,0:T(8,128)(2,1)} %bitcast.3, f32[32,256]{1,0:T(8,128)} %metric.1), custom_call_target="tpu_custom_call" | custom-call | tf_op jit(solution)/shard_map/force_window/pallas_call | solution.py:453
  78.9 1.9 %copy.11 = bf16[1024,256]{1,0:T(8,128)(2,1)} copy(bf16[1024,256]{1,0:T(8,128)(2,1)} %get-tuple-element.12) | data formatting | bytes 1048576
  80.8 1.2 %copy.12 = f32[32]{0:T(128)} copy(f32[32]{0:T(128)} %bitcast.5) | data formatting | bytes 256
  82.0 1.6 %copy.13 = f32[256,128]{1,0:T(8,128)} copy(f32[256,128]{1,0:T(8,128)} %get-tuple-element.14) | data formatting | bytes 262144

commit v3 on v2

--- a/solution.py
+++ b/solution.py
@@ -121,26 +121,24 @@
         return lax.rem(z + d + NZ, NZ)
 
     SIGN = {"+": 1, "-": -1}
-    xs = {}
-    for d, order in (("+", (0, 1)), ("-", (1, 0))):
-        xs[d] = [
-            send(own_vq(q), vq(x, co, q), **shift("row", NX, x, SIGN[d])) for q in order
-        ]
     cme = yl * 8 + z
     base = {"O": yl * 8, "P": (1 - yl) * 8}
     order = {"+": (0, 1), "-": (1, 0)}
     zs = {}
     zy = []
     for k in range(2):
-        for L in "OP":
+        for L in "PO":
             for d in "+-":
                 h = order[d][k]
                 to = shift("z", NZ, z, SIGN[d])
                 if L == "P":
                     to["ylo"] = 1 - yl
                 zs[L, d, 1, h] = send(own_half(h), occ_half(cme, h), **to)
-        zy.append(send(own_half(k), occ_half(cme, k), **ypair))
-
+    xs = {}
+    for d, quarters in (("+", (0, 1)), ("-", (1, 0))):
+        xs[d] = [
+            send(own_vq(q), vq(x, co, q), **shift("row", NX, x, SIGN[d])) for q in quarters
+        ]
     lane = iota((8, 128), 1)
     subl = iota((8, 128), 0)
     idx = [listed[0, n] for n in range(8)]
@@ -166,6 +164,9 @@
                     send(LSRC, LB.at[a], yhi=lax.rem(yh + dh, NYH), core=lax.rem(co + dc, NCO))
                 )
 
+    for h in range(2):
+        zy.append(send(own_half(h), occ_half(cme, h), **ypair))
+
     def relay(step):
         for k in range(2):
             for L in "OP":
@@ -379,22 +380,26 @@
     IL = {"O": 0, "P": 1}
     ID = {"+": 0, "-": 1}
     fs = {}
-    for L in "OP":
+    def send3(L, d, h):
+        i, j = IL[L], ID[d]
+        fs[L, d, 3, h] = send(S3.at[i, j, h], R3.at[i, j, h], **shift("z", NZ, z, SIGN[d]))
+
+    for L in "PO":
+        for d in "+-":
+            v = partial(base[L] + zat(3 * SIGN[d]))
+            for h in range(2):
+                S3[IL[L], ID[d], h] = v[h * 128 : (h + 1) * 128].astype(BF)
+            send3(L, d, order[d][1])
+    for L in "PO":
         v = partial(base[L] + zat(4))
         for d in "+-":
             h = order[d][0]
             i, j = IL[L], ID[d]
             S4[i, j] = v[h * 128 : (h + 1) * 128].astype(BF)
             fs[L, d, 4] = send(S4.at[i, j], R4.at[i, j], **shift("z", NZ, z, 2 * SIGN[d]))
-    for L in "OP":
+    for L in "PO":
         for d in "+-":
-            i, j = IL[L], ID[d]
-            v = partial(base[L] + zat(3 * SIGN[d]))
-            for h in order[d]:
-                S3[i, j, h] = v[h * 128 : (h + 1) * 128].astype(BF)
-                fs[L, d, 3, h] = send(
-                    S3.at[i, j, h], R3.at[i, j, h], **shift("z", NZ, z, SIGN[d])
-                )
+            send3(L, d, order[d][0])
     for dist in (2, -2, 1, -1, 0):
         for L in "OP":
             FP[base[L] + zat(dist)] = partial(base[L] + zat(dist))
@@ -404,7 +409,7 @@
         fy.append(send(SY.at[h], RY.at[h], **ypair))
 
     for k in (1, 0):
-        for L in "OP":
+        for L in "PO":
             for d in "+-":
                 i, j, s = IL[L], ID[d], SIGN[d]
                 h = order[d][k]
@@ -417,7 +422,7 @@
                 S2[i, j, h] = v.astype(BF)
                 fs[L, d, 2, h] = send(S2.at[i, j, h], R2.at[i, j, h], **shift("z", NZ, z, s))
     for k in (1, 0):
-        for L in "OP":
+        for L in "PO":
             for d in "+-":
                 i, j, s = IL[L], ID[d], SIGN[d]
                 h = order[d][k]

time: 83.8 us -> 82.6 us (0.986)
  Pallas kernels: 78.3 us -> 77.1 us
    pallas_call x1, Pallas kernels: 78.3 us -> 77.1 us  [on_device(): pl.pallas_call(body, out_shape=(jax.ShapeDtypeStruct((1024, 256), BF), ja...]
where the time goes in v3:
time: 82.6 us; the launch traced here: 82.4 us
  Pallas kernels  77.1 us (93%)
  local copies, waits for them, and re-layouts  4.6 us (6%)
    pallas_call x1, Pallas kernels, on_device(): pl.pallas_call(body, out_shape=(jax.ShapeDtypeStruct((1024, 256), BF), ja...  77.1 us
    unnamed x3, local copies, waits for them, and re-layouts  4.6 us

profile of v3, /device:TPU:2, one launch (start us, length us, event | category | flops | bytes accessed | tf_op | source)
XLA Modules:
  0.0 82.4 jit_solution(15511067674616388002)
XLA Ops:
  0.6 77.1 %force_window.1 = (bf16[1024,256]{1,0:T(8,128)(2,1)}, f32[1,32]{1,0:T(1,128)}, f32[256,128]{1,0:T(8,128)}) custom-call(s32[1,8]{1,0:T(1,128)} %bitcast.4, bf16[1024,256]{1,0:T(8,128)(2,1)} %occ.1, bf16[1024,256]{1,0:T(8,128)(2,1)} %virt.1, bf16[32,8,4096]{2,1,0:T(8,128)(2,1)} %bitcast.3, f32[32,256]{1,0:T(8,128)} %metric.1), custom_call_target="tpu_custom_call" | custom-call | tf_op jit(solution)/shard_map/force_window/pallas_call | solution.py:458
  77.8 1.9 %copy.11 = bf16[1024,256]{1,0:T(8,128)(2,1)} copy(bf16[1024,256]{1,0:T(8,128)(2,1)} %get-tuple-element.12) | data formatting | bytes 1048576
  79.6 1.2 %copy.12 = f32[32]{0:T(128)} copy(f32[32]{0:T(128)} %bitcast.5) | data formatting | bytes 256
  80.8 1.6 %copy.13 = f32[256,128]{1,0:T(8,128)} copy(f32[256,128]{1,0:T(8,128)} %get-tuple-element.14) | data formatting | bytes 262144

commit v4 on v3

--- a/solution.py
+++ b/solution.py
@@ -10,7 +10,7 @@
 BF = jnp.bfloat16
 F32 = jnp.float32
 NX, NYL, NZ, NYH, NCO = 4, 2, 8, 4, 2
-NCOPY = 160
+NCOPY = 208
 
 
 def iota(shape, dim):
@@ -44,7 +44,7 @@
 def body(
     listed, occ, virt, ints, metric, prod_out, coeff_out, force_out,
     VIRT, OCC, AV, FL, ROWS, PR, CSRC, CZX, CY, ACC, SCB, LSRC, LB,
-    BV, SB, RB, ST, RT, FP, S4, R4, S3, R3, S2, R2, S1, R1, SY, RY, ssem, rsem, lsem,
+    BV, SB, RB, ST, RT, FP, SS, RR, SY, RY, ssem, rsem, lsem, ready,
 ):
     x = lax.axis_index("row")
     yl = lax.axis_index("ylo")
@@ -97,7 +97,13 @@
         for dx in range(NX) for dz in range(NZ) if dx or dz
     ]
     diag = [{"ylo": 1 - yl, "z": lax.rem(z + d + NZ, NZ)} for d in (1, -1)]
-    peers = zx + diag + list(ypeers())
+    peers = [shift("row", NX, x, d) for d in (1, -1)]
+    peers += [shift("z", NZ, z, d) for d in (1, -1, 2, -2)]
+    peers += diag + [ypair]
+    peers += [
+        {"yhi": lax.rem(yh + dh, NYH), "core": lax.rem(co + dc, NCO)}
+        for dh in range(NYH) for dc in range(NCO) if dh or dc
+    ]
     for p in peers:
         pl.semaphore_signal(barrier, inc=1, device_id=p, device_id_type=MESH)
     pl.semaphore_wait(barrier, len(peers))
@@ -154,15 +160,16 @@
     for n in range(8):
         hit = (subl == own[n]) & (lane // 4 == a * 2 + rank[n])
         table = table + jnp.where(hit, (pos[n] + 1).astype(F32), 0.0)
-    LSRC[...] = table
-    LB[a] = table
+    for o in range(8):
+        LSRC[o] = table[o : o + 1, :]
+    LB[a] = LSRC[a]
     lab = []
     for dh in range(NYH):
         for dc in range(NCO):
             if dh or dc:
-                lab.append(
-                    send(LSRC, LB.at[a], yhi=lax.rem(yh + dh, NYH), core=lax.rem(co + dc, NCO))
-                )
+                h2 = lax.rem(yh + dh, NYH)
+                c2 = lax.rem(co + dc, NCO)
+                lab.append(send(LSRC.at[h2 * 2 + c2], LB.at[a], yhi=h2, core=c2))
 
     for h in range(2):
         zy.append(send(own_half(h), occ_half(cme, h), **ypair))
@@ -225,6 +232,10 @@
         for d in "+-":
             zs[L, d, 4, order[d][0]].wait_recv()
         acc = mm(base[L] + zat(4), acc)
+    for d in range(1, NX):
+        pl.semaphore_signal(
+            ready, inc=1, device_id=shift("row", NX, x, d), device_id_type=MESH
+        )
     PR[...] = acc.astype(BF)
     for q in range(2):
         ROWS[q] = acc[:, q * 128 : (q + 1) * 128]
@@ -235,7 +246,7 @@
     labels = LB[0]
     for o in range(1, 8):
         labels = labels + LB[o]
-    labels = jnp.sum(jnp.where(subl == a, labels, 0.0), axis=0, keepdims=True)[:, 0:64]
+    labels = labels[:, 0:64]
     square = jnp.broadcast_to(labels, (64, 64))
     labels_down = jnp.sum(
         jnp.where(iota((64, 64), 0) == iota((64, 64), 1), square, 0.0), axis=1, keepdims=True
@@ -304,34 +315,33 @@
     sub32 = iota((32, 128), 0)
     spread = jnp.where(lane32 == sub32 + lax.rem(a, 4) * 32, part, 0.0)
     spread = jnp.sum(spread, axis=0, keepdims=True)
-    coeff = jnp.where(subl == a // 4, jnp.broadcast_to(spread, (8, 128)), 0.0)
-
-    def exchange(k, value, buf, slot, targets, n):
+
+    def exchange(k, value, buf, slot, targets):
         CSRC[k] = value
         buf[slot] = value
-        cs = [send(CSRC.at[k], buf.at[slot], **t) for t in targets]
-        for c in cs:
+        for c in [send(CSRC.at[k], buf.at[slot], **t) for t in targets]:
             c.wait_recv()
-        total = buf[0]
-        for i in range(1, n):
-            total = total + buf[i]
-        return total
-
-    coeff = exchange(0, coeff, CZX, x * 8 + z, zx, NX * NZ)
-    pfwd = []
-    for c, d in zip(pfar, (1, 3, 2)):
-        c.wait_recv()
-        o = lax.rem(yh + NYH - d, NYH) * 2 + co
-        pfwd.append(send(prow(o), prow(o), **partner))
-    coeff = exchange(1, coeff, CY, yl * 8 + a, list(ypeers()), 16)
-
-    row = jnp.sum(jnp.where(subl == a // 4, coeff, 0.0), axis=0, keepdims=True)
+
+    pl.semaphore_wait(ready, NX - 1)
+    exchange(0, spread, CZX, x * 8 + z, zx)
+    total = CZX[0]
+    for i in range(1, NX * NZ):
+        total = total + CZX[i]
+    exchange(1, total, CY, yl * 8 + a, list(ypeers()))
+    halves = []
+    for first in (0, 4):
+        total = CY[first]
+        for i in (1, 2, 3, 8, 9, 10, 11):
+            total = total + CY[first + i]
+        halves.append(total)
+
+    row = jnp.where(a // 4 == 0, halves[0], halves[1])
     mine = jnp.zeros((1, 32), F32)
     for k in range(4):
         mine = mine + jnp.where(lax.rem(a, 4) == k, row[:, k * 32 : (k + 1) * 32], 0.0)
     coeff_out[...] = mine
 
-    scr = metric[:, 0:128] * coeff[0:1, :] + metric[:, 128:256] * coeff[1:2, :]
+    scr = metric[:, 0:128] * halves[0] + metric[:, 128:256] * halves[1]
     scr = jnp.sum(scr, axis=1, keepdims=True)
     SCB[...] = jnp.broadcast_to(scr, (32, 128))
 
@@ -371,6 +381,7 @@
     rows_from_tiles(FL, ROWS)
     deriv = jnp.concatenate([ROWS[0], ROWS[1]], axis=1).astype(BF)
 
+    order4 = {"+": (0, 1, 2, 3), "-": (2, 3, 0, 1)}
     def partial(i):
         return lax.dot_general(
             VIRT[pl.ds(pl.multiple_of(i * 256, 256), 256), :], deriv,
@@ -380,72 +391,66 @@
     IL = {"O": 0, "P": 1}
     ID = {"+": 0, "-": 1}
     fs = {}
-    def send3(L, d, h):
-        i, j = IL[L], ID[d]
-        fs[L, d, 3, h] = send(S3.at[i, j, h], R3.at[i, j, h], **shift("z", NZ, z, SIGN[d]))
-
-    for L in "PO":
-        for d in "+-":
-            v = partial(base[L] + zat(3 * SIGN[d]))
-            for h in range(2):
-                S3[IL[L], ID[d], h] = v[h * 128 : (h + 1) * 128].astype(BF)
-            send3(L, d, order[d][1])
-    for L in "PO":
-        v = partial(base[L] + zat(4))
-        for d in "+-":
-            h = order[d][0]
-            i, j = IL[L], ID[d]
-            S4[i, j] = v[h * 128 : (h + 1) * 128].astype(BF)
-            fs[L, d, 4] = send(S4.at[i, j], R4.at[i, j], **shift("z", NZ, z, 2 * SIGN[d]))
-    for L in "PO":
-        for d in "+-":
-            send3(L, d, order[d][0])
+    def hop(st, L, d, k, got=None):
+        i, j, s = IL[L], ID[d], SIGN[d]
+        h = order4[d][k]
+        v = FP[base[L] + zat(st * s), h * 64 : (h + 1) * 64, :]
+        if got is not None:
+            fs[L, d, st + 1, k].wait_recv()
+            v = v + RR[st, i, j, k].astype(F32)
+        SS[st - 1, i, j, k] = v.astype(BF)
+        to = shift("z", NZ, z, s)
+        if st == 1 and L == "P":
+            to["ylo"] = 1 - yl
+        fs[L, d, st, k] = send(SS.at[st - 1, i, j, k], RR.at[st - 1, i, j, k], **to)
+
+    def hops(st, ks, got):
+        for k in ks:
+            for L in "PO":
+                for d in "+-":
+                    hop(st, L, d, k, got)
+
+    def fill(dist):
+        for L in "PO":
+            FP[base[L] + zat(dist)] = partial(base[L] + zat(dist))
+
+    fill(4)
+    hops(4, (0, 1), None)
+    fill(3)
+    fill(-3)
+    hops(3, (2, 3), None)
     for dist in (2, -2, 1, -1, 0):
-        for L in "OP":
-            FP[base[L] + zat(dist)] = partial(base[L] + zat(dist))
+        fill(dist)
+    pfwd = []
+    for c, d in zip(pfar, (1, 3, 2)):
+        c.wait_recv()
+        o = lax.rem(yh + NYH - d, NYH) * 2 + co
+        pfwd.append(send(prow(o), prow(o), **partner))
     fy = []
     for h in range(2):
         SY[h] = FP[base["P"] + z, h * 128 : (h + 1) * 128, :].astype(BF)
         fy.append(send(SY.at[h], RY.at[h], **ypair))
 
-    for k in (1, 0):
-        for L in "PO":
-            for d in "+-":
-                i, j, s = IL[L], ID[d], SIGN[d]
-                h = order[d][k]
-                v = FP[base[L] + zat(2 * s), h * 128 : (h + 1) * 128, :]
-                fs[L, d, 3, h].wait_recv()
-                v = v + R3[i, j, h].astype(F32)
-                if k == 0:
-                    fs[L, d, 4].wait_recv()
-                    v = v + R4[i, j].astype(F32)
-                S2[i, j, h] = v.astype(BF)
-                fs[L, d, 2, h] = send(S2.at[i, j, h], R2.at[i, j, h], **shift("z", NZ, z, s))
-    for k in (1, 0):
-        for L in "PO":
-            for d in "+-":
-                i, j, s = IL[L], ID[d], SIGN[d]
-                h = order[d][k]
-                v = FP[base[L] + zat(s), h * 128 : (h + 1) * 128, :]
-                fs[L, d, 2, h].wait_recv()
-                v = v + R2[i, j, h].astype(F32)
-                S1[i, j, h] = v.astype(BF)
-                to = shift("z", NZ, z, s)
-                if L == "P":
-                    to["ylo"] = 1 - yl
-                fs[L, d, 1, h] = send(S1.at[i, j, h], R1.at[i, j, h], **to)
+    hops(3, (0, 1), True)
+    hops(2, (2, 3), True)
+    hops(2, (0, 1), True)
+    hops(1, (2, 3), True)
+    hops(1, (0, 1), True)
     pown.wait()
     pcore.wait_recv()
     for c in pfwd:
         c.wait_recv()
-    for h in range(2):
-        fy[h].wait_recv()
-        v = FP[base["O"] + z, h * 128 : (h + 1) * 128, :] + RY[h].astype(F32)
+    for c in fy:
+        c.wait_recv()
+    for h in (2, 3, 0, 1):
+        v = FP[base["O"] + z, h * 64 : (h + 1) * 64, :]
+        v = v + RY[h // 2, (h % 2) * 64 : (h % 2) * 64 + 64, :].astype(F32)
         for L in "OP":
             for d in "+-":
-                fs[L, d, 1, h].wait_recv()
-                v = v + R1[IL[L], ID[d], h].astype(F32)
-        force_out[h * 128 : (h + 1) * 128, :] = v
+                k = order4[d].index(h)
+                fs[L, d, 1, k].wait_recv()
+                v = v + RR[0, IL[L], ID[d], k].astype(F32)
+        force_out[h * 64 : (h + 1) * 64, :] = v
     for c in started:
         c.wait_send()
     assert count[0] <= NCOPY
@@ -471,32 +476,27 @@
             vm((256, 128), F32),
             vm((2, 128, 128), F32),
             vm((128, 256), BF),
-            vm((2, 8, 128), F32),
-            vm((32, 8, 128), F32),
-            vm((16, 8, 128), F32),
+            vm((2, 1, 128), F32),
+            vm((32, 1, 128), F32),
+            vm((16, 1, 128), F32),
             vm((32, 8, 128), F32),
             vm((32, 128), F32),
-            vm((8, 128), F32),
-            vm((8, 8, 128), F32),
+            vm((8, 1, 128), F32),
+            vm((8, 1, 128), F32),
             vm((8, 4096), F32),
             vm((8, 8, 1024), BF),
             vm((8, 8, 1024), BF),
             vm((8, 8, 1024), BF),
             vm((8, 8, 1024), BF),
             vm((16, 256, 128), F32),
-            vm((2, 2, 128, 128), BF),
-            vm((2, 2, 128, 128), BF),
-            vm((2, 2, 2, 128, 128), BF),
-            vm((2, 2, 2, 128, 128), BF),
-            vm((2, 2, 2, 128, 128), BF),
-            vm((2, 2, 2, 128, 128), BF),
-            vm((2, 2, 2, 128, 128), BF),
-            vm((2, 2, 2, 128, 128), BF),
+            vm((4, 2, 2, 4, 64, 128), BF),
+            vm((4, 2, 2, 4, 64, 128), BF),
             vm((2, 128, 128), BF),
             vm((2, 128, 128), BF),
             pltpu.SemaphoreType.DMA((NCOPY,)),
             pltpu.SemaphoreType.DMA((NCOPY,)),
             pltpu.SemaphoreType.DMA((5,)),
+            pltpu.SemaphoreType.REGULAR,
         ],
         compiler_params=pltpu.CompilerParams(
             collective_id=0, has_side_effects=True, vmem_limit_bytes=60 << 20

time: 82.6 us -> 78 us (0.944)
  the two profiles are of different devices: /device:TPU:2 before, /device:TPU:64 now
where the time goes in v4:
time: 78 us; the launch traced here: 77.7 us
  Pallas kernels  72.5 us (93%)
  local copies, waits for them, and re-layouts  4.6 us (6%)
    pallas_call x1, Pallas kernels, on_device(): pl.pallas_call(body, out_shape=(jax.ShapeDtypeStruct((1024, 256), BF), ja...  72.5 us
    unnamed x3, local copies, waits for them, and re-layouts  4.6 us

profile of v4, /device:TPU:64, one launch (start us, length us, event | category | flops | bytes accessed | tf_op | source)
XLA Modules:
  0.0 77.7 jit_solution(1106693670439491662)
XLA Ops:
  0.6 72.5 %force_window.1 = (bf16[1024,256]{1,0:T(8,128)(2,1)}, f32[1,32]{1,0:T(1,128)}, f32[256,128]{1,0:T(8,128)}) custom-call(s32[1,8]{1,0:T(1,128)} %bitcast.4, bf16[1024,256]{1,0:T(8,128)(2,1)} %occ.1, bf16[1024,256]{1,0:T(8,128)(2,1)} %virt.1, bf16[32,8,4096]{2,1,0:T(8,128)(2,1)} %bitcast.3, f32[32,256]{1,0:T(8,128)} %metric.1), custom_call_target="tpu_custom_call" | custom-call | tf_op jit(solution)/shard_map/force_window/pallas_call | solution.py:463
  73.1 1.9 %copy.11 = bf16[1024,256]{1,0:T(8,128)(2,1)} copy(bf16[1024,256]{1,0:T(8,128)(2,1)} %get-tuple-element.12) | data formatting | bytes 1048576
  75.0 1.2 %copy.12 = f32[32]{0:T(128)} copy(f32[32]{0:T(128)} %bitcast.5) | data formatting | bytes 256
  76.1 1.6 %copy.13 = f32[256,128]{1,0:T(8,128)} copy(f32[256,128]{1,0:T(8,128)} %get-tuple-element.14) | data formatting | bytes 262144

commit v5 on v4

--- a/solution.py
+++ b/solution.py
@@ -454,6 +454,12 @@
     for c in started:
         c.wait_send()
     assert count[0] <= NCOPY
+
+
+def hand_out(p, c, f, p_out, c_out, f_out):
+    p_out[...] = p[...]
+    c_out[...] = c[...]
+    f_out[...] = f[...]
 
 
 def on_device(green_occ, green_virt, integrals, listed, metric):
@@ -505,7 +511,17 @@
     )(
         listed.reshape(1, 8), green_occ, green_virt, integrals.reshape(32, 8, 4096), metric
     )
-    return product, coeff.reshape(32), force
+    return pl.pallas_call(
+        hand_out,
+        out_shape=(
+            jax.ShapeDtypeStruct((1024, 256), BF),
+            jax.ShapeDtypeStruct((32,), F32),
+            jax.ShapeDtypeStruct((256, 128), F32),
+        ),
+        in_specs=[inv] * 3,
+        out_specs=(inv, inv, inv),
+        name="hand_out",
+    )(product, coeff.reshape(32), force)
 
 
 def solution(mesh):

time: 78 us -> 75.2 us (0.964)
  local copies, waits for them, and re-layouts: 4.6 us -> 0 us
  Pallas kernels: 72.5 us -> 74.4 us
    unnamed x3 -> x0, local copies, waits for them, and re-layouts: 4.6 us -> none
    pallas_call x0 -> x1, Pallas kernels: none -> 1.93 us  [on_device(): pl.pallas_call(hand_out, out_shape=(jax.ShapeDtypeStruct((1024, 256), BF)...]
where the time goes in v5:
time: 75.2 us; the launch traced here: 75 us
  Pallas kernels  74.4 us (99%)
    pallas_call x1, Pallas kernels, on_device(): pl.pallas_call(body, out_shape=(jax.ShapeDtypeStruct((1024, 256), BF), ja...  72.5 us
    pallas_call x1, Pallas kernels, on_device(): pl.pallas_call(hand_out, out_shape=(jax.ShapeDtypeStruct((1024, 256), BF)...  1.93 us

profile of v5, /device:TPU:64, one launch (start us, length us, event | category | flops | bytes accessed | tf_op | source)
XLA Modules:
  0.0 75.0 jit_solution(255673135107787332)
XLA Ops:
  0.6 72.5 %force_window.1 = (bf16[1024,256]{1,0:T(8,128)(2,1)}, f32[1,32]{1,0:T(1,128)}, f32[256,128]{1,0:T(8,128)}) custom-call(s32[1,8]{1,0:T(1,128)} %bitcast.5, bf16[1024,256]{1,0:T(8,128)(2,1)} %occ.1, bf16[1024,256]{1,0:T(8,128)(2,1)} %virt.1, bf16[32,8,4096]{2,1,0:T(8,128)(2,1)} %bitcast.3, f32[32,256]{1,0:T(8,128)} %metric.1), custom_call_target="tpu_custom_call" | custom-call | tf_op jit(solution)/shard_map/force_window/pallas_call | solution.py:469
  73.1 1.9 %hand_out.1 = (bf16[1024,256]{1,0:T(8,128)(2,1)}, f32[32]{0:T(128)}, f32[256,128]{1,0:T(8,128)}) custom-call(bf16[1024,256]{1,0:T(8,128)(2,1)} %get-tuple-element.6.p, f32[32]{0:T(128)} %bitcast.4, f32[256,128]{1,0:T(8,128)} %get-tuple-element.8.f), custom_call_target="tpu_custom_call" | custom-call | tf_op jit(solution)/shard_map/hand_out/pallas_call | solution.py:514

commit v6 on v5

--- a/solution.py
+++ b/solution.py
@@ -106,6 +106,23 @@
     ]
     for p in peers:
         pl.semaphore_signal(barrier, inc=1, device_id=p, device_id_type=MESH)
+    lane = iota((8, 128), 1)
+    subl = iota((8, 128), 0)
+    idx = [listed[0, n] for n in range(8)]
+    own = [lax.shift_right_logical(v, 3) for v in idx]
+    pos = [jnp.bitwise_and(v, 7) for v in idx]
+    rank = []
+    for n in range(8):
+        r = jnp.int32(0)
+        for m in range(n):
+            r = r + jnp.where(own[m] == own[n], 1, 0).astype(jnp.int32)
+        rank.append(r)
+    table = jnp.zeros((8, 128), F32)
+    for n in range(8):
+        hit = (subl == own[n]) & (lane // 4 == a * 2 + rank[n])
+        table = table + jnp.where(hit, (pos[n] + 1).astype(F32), 0.0)
+    for o in range(8):
+        LSRC[o] = table[o : o + 1, :]
     pl.semaphore_wait(barrier, len(peers))
 
     def vq(r, half, quarter):
@@ -145,23 +162,6 @@
         xs[d] = [
             send(own_vq(q), vq(x, co, q), **shift("row", NX, x, SIGN[d])) for q in quarters
         ]
-    lane = iota((8, 128), 1)
-    subl = iota((8, 128), 0)
-    idx = [listed[0, n] for n in range(8)]
-    own = [lax.shift_right_logical(v, 3) for v in idx]
-    pos = [jnp.bitwise_and(v, 7) for v in idx]
-    rank = []
-    for n in range(8):
-        r = jnp.int32(0)
-        for m in range(n):
-            r = r + jnp.where(own[m] == own[n], 1, 0).astype(jnp.int32)
-        rank.append(r)
-    table = jnp.zeros((8, 128), F32)
-    for n in range(8):
-        hit = (subl == own[n]) & (lane // 4 == a * 2 + rank[n])
-        table = table + jnp.where(hit, (pos[n] + 1).astype(F32), 0.0)
-    for o in range(8):
-        LSRC[o] = table[o : o + 1, :]
     LB[a] = LSRC[a]
     lab = []
     for dh in range(NYH):
@@ -309,7 +309,7 @@
         ACC[p] = s
         return 0
 
-    lax.fori_loop(0, 32, contract, 0, unroll=2)
+    lax.fori_loop(0, 32, contract, 0, unroll=4)
     part = jnp.sum(jnp.sum(ACC[...], axis=1), axis=1, keepdims=True)
     lane32 = iota((32, 128), 1)
     sub32 = iota((32, 128), 0)
@@ -351,7 +351,7 @@
         return tuple(accs[m] + v[:, m * 128 : (m + 1) * 128] * s for m in range(32))
 
     accs = lax.fori_loop(
-        0, 32, weigh, tuple(jnp.zeros((8, 128), F32) for _ in range(32))
+        0, 32, weigh, tuple(jnp.zeros((8, 128), F32) for _ in range(32)), unroll=2
     )
     for m in range(32):
         BV[:, m * 128 : (m + 1) * 128] = accs[m]

time: 75.2 us -> 74.9 us (level)
  no operation moved by 1% of the time
where the time goes in v6:
time: 74.9 us; the launch traced here: 74.7 us
  Pallas kernels  74 us (99%)
    pallas_call x1, Pallas kernels, on_device(): pl.pallas_call(body, out_shape=(jax.ShapeDtypeStruct((1024, 256), BF), ja...  72.1 us
    pallas_call x1, Pallas kernels, on_device(): pl.pallas_call(hand_out, out_shape=(jax.ShapeDtypeStruct((1024, 256), BF)...  1.93 us

profile of v6, /device:TPU:64, one launch (start us, length us, event | category | flops | bytes accessed | tf_op | source)
XLA Modules:
  0.0 74.7 jit_solution(1330377993613218643)
XLA Ops:
  0.6 72.1 %force_window.1 = (bf16[1024,256]{1,0:T(8,128)(2,1)}, f32[1,32]{1,0:T(1,128)}, f32[256,128]{1,0:T(8,128)}) custom-call(s32[1,8]{1,0:T(1,128)} %bitcast.5, bf16[1024,256]{1,0:T(8,128)(2,1)} %occ.1, bf16[1024,256]{1,0:T(8,128)(2,1)} %virt.1, bf16[32,8,4096]{2,1,0:T(8,128)(2,1)} %bitcast.3, f32[32,256]{1,0:T(8,128)} %metric.1), custom_call_target="tpu_custom_call" | custom-call | tf_op jit(solution)/shard_map/force_window/pallas_call | solution.py:469
  72.7 1.9 %hand_out.1 = (bf16[1024,256]{1,0:T(8,128)(2,1)}, f32[32]{0:T(128)}, f32[256,128]{1,0:T(8,128)}) custom-call(bf16[1024,256]{1,0:T(8,128)(2,1)} %get-tuple-element.6.p, f32[32]{0:T(128)} %bitcast.4, f32[256,128]{1,0:T(8,128)} %get-tuple-element.8.f), custom_call_target="tpu_custom_call" | custom-call | tf_op jit(solution)/shard_map/hand_out/pallas_call | solution.py:514
